TPU v7x, 512 devices: a whole 4x4x16 slice. The times are simulated.
512 devices in a mesh: slab: 128 (over y_lo, z, x), col: 4 (over y_hi, core).
Axes of the slice: x: 4, y: 4 (y_hi: 2, y_lo: 2; y = y_hi * 2 + y_lo), z: 16, core: 2. Of those that a mesh axis runs over, the one named last changes fastest.
Arguments:
- offsets: float32 [3, 256, 8, 4, 128], P(None, 'slab', 'col'), may hold values from 0 to 2
- velocity: float32 [3, 256, 8, 4, 128], P(None, 'slab', 'col'), may hold values from -6 to 6
- occupancy: int32 [256, 8, 4], P('slab', 'col'), may hold values from 32 to 128
Outputs:
- new_offsets: float32 [3, 256, 8, 4, 128], P(None, 'slab', 'col')
- new_velocity: float32 [3, 256, 8, 4, 128], P(None, 'slab', 'col')
- density: float32 [256, 8, 4, 128], P('slab', 'col')
All inputs are finite; a program needn't handle non-finite values.
Results may differ from a plain program's by a relative error of at most 0.0001.
Values sent between devices are 32-bit elements; how exact they have to be, the bound alone decides.
No kernel may reach another device: no remote copies, remote signals or barrier semaphores. Data moves between devices by JAX's collectives and lax.ppermute only.
A program may use at most 64 MiB of HBM per device.

v0:
```python
import math

import jax
import jax.numpy as jnp
from jax import lax
from jax.sharding import PartitionSpec as P

STEPS = 2


kernel_norm = 21.0 / (16.0 * math.pi)
sound_speed = 10.0
tait_coef = sound_speed * sound_speed / 7.0
time_step = 0.02
gravity = 1.0
visc_alpha = 0.2
visc_floor = 0.01
cell_edge = 2.0
plane_steps = [(step_x, step_y) for step_x in (-1, 0, 1) for step_y in (-1, 0, 1)]


def with_halo(cells, sides, width):
    for axis, dim in sides:
        count = lax.axis_size(axis)
        ends = count - 1
        head = lax.slice_in_dim(cells, 0, width, axis=dim)
        tail = lax.slice_in_dim(cells, cells.shape[dim] - width, cells.shape[dim], axis=dim)
        cells = jnp.concatenate(
            [
                lax.ppermute(tail, axis, [(i, (i + 1) % count) for i in range(ends)]),
                cells,
                lax.ppermute(head, axis, [((i + 1) % count, i) for i in range(ends)]),
            ],
            axis=dim,
        )
    return cells


def live_slots(count_cells, slot_count):
    slot_rank = jnp.arange(slot_count, dtype=jnp.float32)
    return (slot_rank < count_cells).astype(jnp.float32)


def pair_geometry(target_pos, source_pos, cell_step):
    separation = []
    distance_sq = 0.0
    for axis_num in range(3):
        spacing = (
            target_pos[axis_num][..., :, None]
            - source_pos[axis_num][..., None, :]
            - cell_edge * cell_step[axis_num]
        )
        separation.append(spacing)
        distance_sq = distance_sq + spacing * spacing
    return (separation, distance_sq)


def pressure_of(density):
    cubed = density * density * density
    return tait_coef * (cubed * cubed * density - 1.0)


def density_terms(target_pos, source_pos, source_live, cell_step, particle_mass):
    separation, distance_sq = pair_geometry(target_pos, source_pos, cell_step)
    radius = jnp.sqrt(distance_sq)
    inside = jnp.maximum(1.0 - 0.5 * radius, 0.0)
    inside_sq = inside * inside
    weight = kernel_norm * inside_sq * inside_sq * (2.0 * radius + 1.0)
    return particle_mass * jnp.sum(weight * source_live[..., None, :], axis=-1)


def force_terms(target, source, cell_step, particle_mass):
    target_pos, target_vel, target_density, target_pressure = target
    source_pos, source_vel, source_density, source_live = source
    source_density = jnp.maximum(source_density, particle_mass * kernel_norm)
    source_pressure = pressure_of(source_density)
    separation, distance_sq = pair_geometry(target_pos, source_pos, cell_step)
    inside = jnp.maximum(1.0 - 0.5 * jnp.sqrt(distance_sq), 0.0)
    slope = -5.0 * kernel_norm * inside * inside * inside
    approach = 0.0
    for axis_num in range(3):
        approach = (
            approach
            + (target_vel[axis_num][..., :, None] - source_vel[axis_num][..., None, :])
            * separation[axis_num]
        )
    closing = jnp.minimum(approach, 0.0) / (distance_sq + visc_floor)
    mean_density = 0.5 * (target_density[..., :, None] + source_density[..., None, :])
    viscous = -visc_alpha * sound_speed * closing / mean_density
    target_ratio = target_pressure / (target_density * target_density)
    source_ratio = source_pressure / (source_density * source_density)
    strength = (
        particle_mass
        * source_live[..., None, :]
        * (target_ratio[..., :, None] + source_ratio[..., None, :] + viscous)
        * slope
    )
    return jnp.stack([-jnp.sum(strength * separation[axis_num], axis=-1) for axis_num in range(3)])


def neighbour_total(term_fn, source_arrays, cells_x, cells_y):
    padded = [
        jnp.pad(source_arr, ((0, 0), (0, 0), (0, 0), (1, 1), (0, 0)))
        for source_arr in source_arrays
    ]
    cells_z = source_arrays[0].shape[3]
    slot_count = source_arrays[0].shape[4]
    z_steps = jnp.repeat(jnp.array([-1.0, 0.0, 1.0], dtype=jnp.float32), slot_count)
    running = None
    for step_x, step_y in plane_steps:
        sliced = [
            jnp.concatenate(
                [
                    source_arr[
                        :,
                        1 + step_x : 1 + step_x + cells_x,
                        1 + step_y : 1 + step_y + cells_y,
                        1 + step_z : 1 + step_z + cells_z,
                    ]
                    for step_z in (-1, 0, 1)
                ],
                axis=-1,
            )
            for source_arr in padded
        ]
        contribution = term_fn(sliced, (step_x, step_y, z_steps))
        running = contribution if running is None else running + contribution
    return running


def density_field(source_pos, source_live, particle_mass):
    cells_x = source_pos.shape[1] - 2
    cells_y = source_pos.shape[2] - 2
    target_pos = source_pos[:, 1 : 1 + cells_x, 1 : 1 + cells_y]
    target_live = source_live[0, 1 : 1 + cells_x, 1 : 1 + cells_y]

    def term_fn(sliced, cell_step):
        return density_terms(target_pos, sliced[0], sliced[1][0], cell_step, particle_mass)

    summed = neighbour_total(term_fn, [source_pos, source_live], cells_x, cells_y)
    return (summed + (1.0 - target_live) * particle_mass * kernel_norm)[None]


def force_field(source_state, source_density, source_live, particle_mass):
    cells_x = source_state.shape[1] - 2
    cells_y = source_state.shape[2] - 2
    inner = source_state[:, 1 : 1 + cells_x, 1 : 1 + cells_y]
    target_density = jnp.maximum(
        source_density[0, 1 : 1 + cells_x, 1 : 1 + cells_y], particle_mass * kernel_norm
    )
    target = (inner[0:3], inner[3:6], target_density, pressure_of(target_density))

    def term_fn(sliced, cell_step):
        return force_terms(
            target,
            (sliced[0][0:3], sliced[0][3:6], sliced[1][0], sliced[2][0]),
            cell_step,
            particle_mass,
        )

    return neighbour_total(term_fn, [source_state, source_density, source_live], cells_x, cells_y)


def advance(particle_state, acceleration, own_live):
    gravity_pull = jnp.array([0.0, 0.0, gravity], dtype=jnp.float32)[:, None, None, None, None]
    new_vel = particle_state[3:6] + time_step * (acceleration - gravity_pull)
    new_pos = particle_state[0:3] + time_step * new_vel
    updated = jnp.concatenate([new_pos, new_vel], axis=0)
    return own_live * updated + (1.0 - own_live) * particle_state


def state_ghosts(particle_state, count_cells, width):
    return (
        with_halo(particle_state, (("slab", 1), ("col", 2)), width),
        with_halo(count_cells, (("slab", 1), ("col", 2)), width),
    )


def density_ghosts(density):
    return with_halo(density, (("slab", 1), ("col", 2)), 1)


def per_device(offsets, velocity, occupancy):
    slot_count = offsets.shape[-1]
    particle_mass = 8.0 / slot_count
    particle_state = jnp.concatenate([offsets, velocity], axis=0)
    count_cells = occupancy.astype(jnp.float32)[None, :, :, :, None]
    own_live = live_slots(count_cells, slot_count)
    density = None
    for section_num in range(STEPS):
        wide_state, wide_count = state_ghosts(particle_state, count_cells, 1)
        wide_live = live_slots(wide_count, slot_count)
        density = density_field(wide_state[0:3], wide_live, particle_mass)
        wide_density = density_ghosts(density)
        acceleration = force_field(wide_state, wide_density, wide_live, particle_mass)
        particle_state = advance(particle_state, acceleration, own_live)
    return (particle_state[0:3], particle_state[3:6], density[0])


def solution(mesh):
    placed = (
        P(None, "slab", "col", None, None),
        P(None, "slab", "col", None, None),
        P("slab", "col", None),
    )
    return jax.shard_map(
        per_device,
        mesh=mesh,
        in_specs=placed,
        out_specs=(
            P(None, "slab", "col", None, None),
            P(None, "slab", "col", None, None),
            P("slab", "col", None, None),
        ),
        check_vma=False,
    )
```

profile of v0, /device:TPU:24, one launch (start us, length us, event | category | flops | bytes accessed | tf_op | source)
XLA Modules:
  0.0 301.6 jit_solution(9858734257818962297)
XLA Ops:
  5.6 12.3 %collective-permute-start.5 = (f32[6,1,2,4,128]{4,3,2,1,0:T(4,128)S(1)}, f32[6,1,2,4,128]{4,3,2,1,0:T(4,128)S(1)}, u32[]{:S(2)}, u32[]{:S(2)}) collective-permute-start(f32[6,1,2,4,128]{4,3,2,1,0:T(4,128)S(1)} %get-tuple-element.416), channel_id=1, source_target_pairs={{4,0},{8,4},{12,8},{16,12},{20,16},{24,20},{28,24},{32,28},{36,32}... | collective-permute-start | bytes 73736 | tf_op jit(solution)/shard_map/ppermute | solution.py:32
  19.9 8.1 %collective-permute-start.1 = (f32[1,1,2,4,1]{3,2,1,4,0:T(2,128)S(1)}, f32[1,1,2,4,1]{3,2,1,4,0:T(2,128)S(1)}, u32[]{:S(2)}, u32[]{:S(2)}) collective-permute-start(f32[1,1,2,4,1]{3,2,1,4,0:T(2,128)S(1)} %get-tuple-element.485), channel_id=1, source_target_pairs={{4,0},{8,4},{12,8},{16,12},{20,16},{24,20},{28,24},{32,28},{36,32}... | collective-permute-start | bytes 104 | tf_op jit(solution)/shard_map/ppermute | solution.py:32
  49.1 9.4 %fusion.5 = (f32[2,2,4,128]{3,2,1,0:T(4,128)S(1)}, f32[2,2,4,128]{3,2,1,0:T(4,128)S(1)}, f32[2,2,4,128]{3,2,1,0:T(4,128)S(1)}) fusion(f32[2,2,4,384]{3,2,1,0:T(4,128)S(1)} %get-tuple-element.495, f32[2,2,4,384]{3,2,1,0:T(4,128)S(1)} %get-tuple-element.339, f32[2,2,4,384]{3,2,1,0:T(4,128)S(1)} %get-tuple-element.340, ...), kind=kLoop, calls=%fused_computation.77 | loop fusion | flops 50325504 | bytes 345600 | tf_op jit(solution)/shard_map/reduce_sum | solution.py:69
  58.5 9.3 %fusion.2 = (f32[2,2,4,128]{3,2,1,0:T(4,128)S(1)}, f32[2,2,4,128]{3,2,1,0:T(4,128)S(1)}, f32[2,2,4,128]{3,2,1,0:T(4,128)S(1)}) fusion(f32[2,2,4,384]{3,2,1,0:T(4,128)S(1)} %get-tuple-element.494, f32[384]{0:T(512)S(1)} %broadcast_bitcast_fusion, f32[2,2,4,384]{3,2,1,0:T(4,128)S(1)} %get-tuple-element.348, f32[2,2,4,128]{3,2,1,0:T(4,128)S(1)} %get-tuple-element.460, ...), kind=kLoop, calls=%fused_computation.74 | loop fusion | flops 49539072 | bytes 345600 | tf_op jit(solution)/shard_map/reduce_sum | solution.py:69
  67.9 10.1 %fusion.20 = (f32[2,2,4,128]{3,2,1,0:T(4,128)S(1)}, f32[2,2,4,128]{3,2,1,0:T(4,128)S(1)}, f32[2,2,4,128]{3,2,1,0:T(4,128)S(1)}) fusion(f32[2,2,4,384]{3,2,1,0:T(4,128)S(1)} %get-tuple-element.500, f32[2,2,4,384]{3,2,1,0:T(4,128)S(1)} %get-tuple-element.357, f32[2,2,4,384]{3,2,1,0:T(4,128)S(1)} %get-tuple-element.358, ...), kind=kLoop, calls=%fused_computation.92 | loop fusion | flops 51111936 | bytes 345600 | tf_op jit(solution)/shard_map/reduce_sum | solution.py:69
  80.0 8.4 %collective-permute-start.9 = (f32[1,1,2,4,128]{4,3,2,1,0:T(4,128)S(1)}, f32[1,1,2,4,128]{4,3,2,1,0:T(4,128)S(1)}, u32[]{:S(2)}, u32[]{:S(2)}) collective-permute-start(f32[1,1,2,4,128]{4,3,2,1,0:T(4,128)S(1)} %get-tuple-element.479), channel_id=1, source_target_pairs={{4,0},{8,4},{12,8},{16,12},{20,16},{24,20},{28,24},{32,28},{36,32}... | collective-permute-start | bytes 12296 | tf_op jit(solution)/shard_map/ppermute | solution.py:32
  91.7 5.3 %collective-permute-start.11 = (f32[1,4,1,4,128]{4,3,2,1,0:T(4,128)S(1)}, f32[1,4,1,4,128]{4,3,2,1,0:T(4,128)S(1)}, u32[]{:S(2)}, u32[]{:S(2)}) collective-permute-start(f32[1,4,1,4,128]{4,3,2,1,0:T(4,128)S(1)} %get-tuple-element.469), channel_id=1, source_target_pairs={{1,0},{2,1},{3,2},{5,4},{6,5},{7,6},{9,8},{10,9},{11,10},{13,12},{... | collective-permute-start | bytes 24584 | tf_op jit(solution)/shard_map/ppermute | solution.py:32
  98.6 7.2 %multiply_reduce_fusion.41 = (f32[2,2,4,128]{3,2,1,0:T(4,128)S(1)}, f32[2,2,4,128]{3,2,1,0:T(4,128)S(1)}, f32[2,2,4,128]{3,2,1,0:T(4,128)S(1)}) fusion(f32[2,2,4,384]{3,2,1,0:T(4,128)S(1)} %get-tuple-element.200, f32[2,2,4,128]{3,2,1,0:T(4,128)S(1)} %get-tuple-element.461, f32[2,2,4,384]{3,2,1,0:T(4,128)S(1)} %fusion.272, ...), kind=kLoop, calls=%fused_computation.316 | loop fusion | flops 33024000 | bytes 312832 | tf_op jit(solution)/shard_map/reduce_sum | solution.py:98
  105.9 7.1 %multiply_reduce_fusion.38 = (f32[2,2,4,128]{3,2,1,0:T(4,128)S(1)}, f32[2,2,4,128]{3,2,1,0:T(4,128)S(1)}, f32[2,2,4,128]{3,2,1,0:T(4,128)S(1)}) fusion(f32[2,2,4,384]{3,2,1,0:T(4,128)S(1)} %get-tuple-element.209, f32[2,2,4,128]{3,2,1,0:T(4,128)S(1)} %get-tuple-element.461, f32[2,2,4,384]{3,2,1,0:T(4,128)S(1)} %get-tuple-element.87, ...), kind=kLoop, calls=%fused_computation.311 | loop fusion | flops 32237568 | bytes 312832 | tf_op jit(solution)/shard_map/reduce_sum | solution.py:98
  113.0 7.2 %multiply_reduce_fusion.36 = (f32[2,2,4,128]{3,2,1,0:T(4,128)S(1)}, f32[2,2,4,128]{3,2,1,0:T(4,128)S(1)}, f32[2,2,4,128]{3,2,1,0:T(4,128)S(1)}) fusion(f32[2,2,4,384]{3,2,1,0:T(4,128)S(1)} %get-tuple-element.215, f32[2,2,4,128]{3,2,1,0:T(4,128)S(1)} %get-tuple-element.461, f32[2,2,4,384]{3,2,1,0:T(4,128)S(1)} %fusion.280, ...), kind=kLoop, calls=%fused_computation.306 | loop fusion | flops 33024000 | bytes 312832 | tf_op jit(solution)/shard_map/reduce_sum | solution.py:98
  120.2 7.0 %fusion.89 = (f32[2,2,4,128]{3,2,1,0:T(4,128)S(1)}, f32[2,2,4,128]{3,2,1,0:T(4,128)S(1)}, f32[2,2,4,128]{3,2,1,0:T(4,128)S(1)}) fusion(f32[2,2,4,384]{3,2,1,0:T(4,128)S(1)} %get-tuple-element.224, f32[2,2,4,128]{3,2,1,0:T(4,128)S(1)} %get-tuple-element.461, f32[2,2,4,384]{3,2,1,0:T(4,128)S(1)} %fusion.281, f32[2,2,4,128]{3,2,1,0:T(4,128)S(1)} %get-tuple-element.91, ...), kind=kLoop, calls=%fused_computation.161 | loop fusion | flops 32237568 | bytes 312832 | tf_op jit(solution)/shard_map/reduce_sum | solution.py:98
  127.3 6.9 %fusion.98 = (f32[2,2,4,128]{3,2,1,0:T(4,128)S(1)}, f32[2,2,4,128]{3,2,1,0:T(4,128)S(1)}, f32[2,2,4,128]{3,2,1,0:T(4,128)S(1)}) fusion(f32[2,2,4,384]{3,2,1,0:T(4,128)S(1)} %get-tuple-element.230, f32[2,2,4,128]{3,2,1,0:T(4,128)S(1)} %get-tuple-element.461, f32[2,2,4,384]{3,2,1,0:T(4,128)S(1)} %fusion.282, f32[2,2,4,128]{3,2,1,0:T(4,128)S(1)} %get-tuple-element.91, ...), kind=kLoop, calls=%fused_computation.170 | loop fusion | flops 31451136 | bytes 312832 | tf_op jit(solution)/shard_map/reduce_sum | solution.py:98
  134.2 7.0 %fusion.108 = (f32[2,2,4,128]{3,2,1,0:T(4,128)S(1)}, f32[2,2,4,128]{3,2,1,0:T(4,128)S(1)}, f32[2,2,4,128]{3,2,1,0:T(4,128)S(1)}) fusion(f32[2,2,4,384]{3,2,1,0:T(4,128)S(1)} %get-tuple-element.236, f32[2,2,4,128]{3,2,1,0:T(4,128)S(1)} %get-tuple-element.461, f32[2,2,4,384]{3,2,1,0:T(4,128)S(1)} %fusion.283, f32[2,2,4,128]{3,2,1,0:T(4,128)S(1)} %get-tuple-element.91, ...), kind=kLoop, calls=%fused_computation.180 | loop fusion | flops 32237568 | bytes 312832 | tf_op jit(solution)/shard_map/reduce_sum | solution.py:98
  141.3 7.2 %multiply_reduce_fusion.28 = (f32[2,2,4,128]{3,2,1,0:T(4,128)S(1)}, f32[2,2,4,128]{3,2,1,0:T(4,128)S(1)}, f32[2,2,4,128]{3,2,1,0:T(4,128)S(1)}) fusion(f32[2,2,4,384]{3,2,1,0:T(4,128)S(1)} %get-tuple-element.242, f32[2,2,4,128]{3,2,1,0:T(4,128)S(1)} %get-tuple-element.461, f32[2,2,4,384]{3,2,1,0:T(4,128)S(1)} %fusion.284, ...), kind=kLoop, calls=%fused_computation.290 | loop fusion | flops 33024000 | bytes 312832 | tf_op jit(solution)/shard_map/reduce_sum | solution.py:98
  148.5 7.1 %multiply_reduce_fusion.25 = (f32[2,2,4,128]{3,2,1,0:T(4,128)S(1)}, f32[2,2,4,128]{3,2,1,0:T(4,128)S(1)}, f32[2,2,4,128]{3,2,1,0:T(4,128)S(1)}) fusion(f32[2,2,4,384]{3,2,1,0:T(4,128)S(1)} %get-tuple-element.248, f32[2,2,4,128]{3,2,1,0:T(4,128)S(1)} %get-tuple-element.461, f32[2,2,4,384]{3,2,1,0:T(4,128)S(1)} %get-tuple-element.477, ...), kind=kLoop, calls=%fused_computation.285 | loop fusion | flops 32237568 | bytes 312832 | tf_op jit(solution)/shard_map/reduce_sum | solution.py:98
  155.7 7.2 %multiply_reduce_fusion.23 = (f32[2,2,4,128]{3,2,1,0:T(4,128)S(1)}, f32[2,2,4,128]{3,2,1,0:T(4,128)S(1)}, f32[2,2,4,128]{3,2,1,0:T(4,128)S(1)}) fusion(f32[2,2,4,384]{3,2,1,0:T(4,128)S(1)} %get-tuple-element.254, f32[2,2,4,128]{3,2,1,0:T(4,128)S(1)} %get-tuple-element.461, f32[2,2,4,384]{3,2,1,0:T(4,128)S(1)} %fusion.285, ...), kind=kLoop, calls=%fused_computation.280 | loop fusion | flops 33024000 | bytes 312832 | tf_op jit(solution)/shard_map/reduce_sum | solution.py:98
  165.0 8.4 %collective-permute-start.13 = (f32[6,1,2,4,128]{4,3,2,1,0:T(4,128)S(1)}, f32[6,1,2,4,128]{4,3,2,1,0:T(4,128)S(1)}, u32[]{:S(2)}, u32[]{:S(2)}) collective-permute-start(f32[6,1,2,4,128]{4,3,2,1,0:T(4,128)S(1)} %get-tuple-element.409), channel_id=1, source_target_pairs={{4,0},{8,4},{12,8},{16,12},{20,16},{24,20},{28,24},{32,28},{36,32}... | collective-permute-start | bytes 73736 | tf_op jit(solution)/shard_map/ppermute | solution.py:32
  176.9 5.4 %collective-permute-start.15 = (f32[6,4,1,4,128]{4,3,2,1,0:T(4,128)S(1)}, f32[6,4,1,4,128]{4,3,2,1,0:T(4,128)S(1)}, u32[]{:S(2)}, u32[]{:S(2)}) collective-permute-start(f32[6,4,1,4,128]{4,3,2,1,0:T(4,128)S(1)} %get-tuple-element.282), channel_id=1, source_target_pairs={{1,0},{2,1},{3,2},{5,4},{6,5},{7,6},{9,8},{10,9},{11,10},{13,12},{... | collective-permute-start | bytes 147464 | tf_op jit(solution)/shard_map/ppermute | solution.py:32
  186.6 9.4 %fusion.41 = (f32[2,2,4,128]{3,2,1,0:T(4,128)S(1)}, f32[2,2,4,128]{3,2,1,0:T(4,128)S(1)}, f32[2,2,4,128]{3,2,1,0:T(4,128)S(1)}) fusion(f32[2,2,4,384]{3,2,1,0:T(4,128)S(1)} %get-tuple-element.312, f32[2,2,4,384]{3,2,1,0:T(4,128)S(1)} %get-tuple-element.313, f32[2,2,4,384]{3,2,1,0:T(4,128)S(1)} %get-tuple-element.311, ...), kind=kLoop, calls=%fused_computation.113 | loop fusion | flops 50325504 | bytes 345600 | tf_op jit(solution)/shard_map/reduce_sum | solution.py:69
  196.0 9.3 %fusion.38 = (f32[2,2,4,128]{3,2,1,0:T(4,128)S(1)}, f32[2,2,4,128]{3,2,1,0:T(4,128)S(1)}, f32[2,2,4,128]{3,2,1,0:T(4,128)S(1)}) fusion(f32[2,2,4,384]{3,2,1,0:T(4,128)S(1)} %get-tuple-element.321, f32[2,2,4,128]{3,2,1,0:T(4,128)S(1)} %get-tuple-element.403, f32[2,2,4,384]{3,2,1,0:T(4,128)S(1)} %get-tuple-element.322, ...), kind=kLoop, calls=%fused_computation.110 | loop fusion | flops 49539072 | bytes 345600 | tf_op jit(solution)/shard_map/reduce_sum | solution.py:69
  205.4 10.1 %fusion.56 = (f32[2,2,4,128]{3,2,1,0:T(4,128)S(1)}, f32[2,2,4,128]{3,2,1,0:T(4,128)S(1)}, f32[2,2,4,128]{3,2,1,0:T(4,128)S(1)}) fusion(f32[2,2,4,384]{3,2,1,0:T(4,128)S(1)} %get-tuple-element.330, f32[2,2,4,384]{3,2,1,0:T(4,128)S(1)} %get-tuple-element.331, f32[2,2,4,384]{3,2,1,0:T(4,128)S(1)} %get-tuple-element.329, ...), kind=kLoop, calls=%fused_computation.128 | loop fusion | flops 51111936 | bytes 345600 | tf_op jit(solution)/shard_map/reduce_sum | solution.py:69
  217.5 8.4 %collective-permute-start.17 = (f32[1,1,2,4,128]{4,3,2,1,0:T(4,128)S(1)}, f32[1,1,2,4,128]{4,3,2,1,0:T(4,128)S(1)}, u32[]{:S(2)}, u32[]{:S(2)}) collective-permute-start(f32[1,1,2,4,128]{4,3,2,1,0:T(4,128)S(1)} %get-tuple-element.474), channel_id=1, source_target_pairs={{4,0},{8,4},{12,8},{16,12},{20,16},{24,20},{28,24},{32,28},{36,32}... | collective-permute-start | bytes 12296 | tf_op jit(solution)/shard_map/ppermute | solution.py:32
  229.3 5.8 %collective-permute-start.19 = (f32[1,4,1,4,128]{4,3,2,1,0:T(4,128)S(1)}, f32[1,4,1,4,128]{4,3,2,1,0:T(4,128)S(1)}, u32[]{:S(2)}, u32[]{:S(2)}) collective-permute-start(f32[1,4,1,4,128]{4,3,2,1,0:T(4,128)S(1)} %get-tuple-element.465), channel_id=1, source_target_pairs={{1,0},{2,1},{3,2},{5,4},{6,5},{7,6},{9,8},{10,9},{11,10},{13,12},{... | collective-permute-start | bytes 24584 | tf_op jit(solution)/shard_map/ppermute | solution.py:32
  236.5 7.2 %multiply_reduce_fusion.20 = (f32[2,2,4,128]{3,2,1,0:T(4,128)S(1)}, f32[2,2,4,128]{3,2,1,0:T(4,128)S(1)}, f32[2,2,4,128]{3,2,1,0:T(4,128)S(1)}) fusion(f32[2,2,4,384]{3,2,1,0:T(4,128)S(1)} %get-tuple-element.134, f32[2,2,4,128]{3,2,1,0:T(4,128)S(1)} %get-tuple-element.405, f32[2,2,4,384]{3,2,1,0:T(4,128)S(1)} %fusion.286, ...), kind=kLoop, calls=%fused_computation.274 | loop fusion | flops 33024000 | bytes 312832 | tf_op jit(solution)/shard_map/reduce_sum | solution.py:98
  243.8 7.1 %multiply_reduce_fusion.17 = (f32[2,2,4,128]{3,2,1,0:T(4,128)S(1)}, f32[2,2,4,128]{3,2,1,0:T(4,128)S(1)}, f32[2,2,4,128]{3,2,1,0:T(4,128)S(1)}) fusion(f32[2,2,4,384]{3,2,1,0:T(4,128)S(1)} %get-tuple-element.143, f32[2,2,4,128]{3,2,1,0:T(4,128)S(1)} %get-tuple-element.405, f32[2,2,4,384]{3,2,1,0:T(4,128)S(1)} %get-tuple-element.78, ...), kind=kLoop, calls=%fused_computation.269 | loop fusion | flops 32237568 | bytes 312832 | tf_op jit(solution)/shard_map/reduce_sum | solution.py:98
  251.0 7.2 %multiply_reduce_fusion.15 = (f32[2,2,4,128]{3,2,1,0:T(4,128)S(1)}, f32[2,2,4,128]{3,2,1,0:T(4,128)S(1)}, f32[2,2,4,128]{3,2,1,0:T(4,128)S(1)}) fusion(f32[2,2,4,384]{3,2,1,0:T(4,128)S(1)} %get-tuple-element.149, f32[2,2,4,128]{3,2,1,0:T(4,128)S(1)} %get-tuple-element.405, f32[2,2,4,384]{3,2,1,0:T(4,128)S(1)} %fusion.294, ...), kind=kLoop, calls=%fused_computation.264 | loop fusion | flops 33024000 | bytes 312832 | tf_op jit(solution)/shard_map/reduce_sum | solution.py:98
  258.2 7.0 %fusion.135 = (f32[2,2,4,128]{3,2,1,0:T(4,128)S(1)}, f32[2,2,4,128]{3,2,1,0:T(4,128)S(1)}, f32[2,2,4,128]{3,2,1,0:T(4,128)S(1)}) fusion(f32[2,2,4,384]{3,2,1,0:T(4,128)S(1)} %get-tuple-element.158, f32[2,2,4,128]{3,2,1,0:T(4,128)S(1)} %get-tuple-element.405, f32[2,2,4,384]{3,2,1,0:T(4,128)S(1)} %fusion.295, f32[2,2,4,128]{3,2,1,0:T(4,128)S(1)} %broadcast_maximum_fusion, ...), kind=kLoop, calls=%fused_computation.207 | loop fusion | flops 32237568 | bytes 312832 | tf_op jit(solution)/shard_map/reduce_sum | solution.py:98
  265.2 6.9 %fusion.144 = (f32[2,2,4,128]{3,2,1,0:T(4,128)S(1)}, f32[2,2,4,128]{3,2,1,0:T(4,128)S(1)}, f32[2,2,4,128]{3,2,1,0:T(4,128)S(1)}) fusion(f32[2,2,4,384]{3,2,1,0:T(4,128)S(1)} %get-tuple-element.164, f32[2,2,4,128]{3,2,1,0:T(4,128)S(1)} %get-tuple-element.405, f32[2,2,4,384]{3,2,1,0:T(4,128)S(1)} %fusion.296, f32[2,2,4,128]{3,2,1,0:T(4,128)S(1)} %broadcast_maximum_fusion, ...), kind=kLoop, calls=%fused_computation.216 | loop fusion | flops 31451136 | bytes 312832 | tf_op jit(solution)/shard_map/reduce_sum | solution.py:98
  272.2 7.0 %fusion.154 = (f32[2,2,4,128]{3,2,1,0:T(4,128)S(1)}, f32[2,2,4,128]{3,2,1,0:T(4,128)S(1)}, f32[2,2,4,128]{3,2,1,0:T(4,128)S(1)}) fusion(f32[2,2,4,384]{3,2,1,0:T(4,128)S(1)} %get-tuple-element.170, f32[2,2,4,128]{3,2,1,0:T(4,128)S(1)} %get-tuple-element.405, f32[2,2,4,384]{3,2,1,0:T(4,128)S(1)} %fusion.297, f32[2,2,4,128]{3,2,1,0:T(4,128)S(1)} %broadcast_maximum_fusion, ...), kind=kLoop, calls=%fused_computation.226 | loop fusion | flops 32237568 | bytes 312832 | tf_op jit(solution)/shard_map/reduce_sum | solution.py:98
  279.3 7.2 %multiply_reduce_fusion.7 = (f32[2,2,4,128]{3,2,1,0:T(4,128)S(1)}, f32[2,2,4,128]{3,2,1,0:T(4,128)S(1)}, f32[2,2,4,128]{3,2,1,0:T(4,128)S(1)}) fusion(f32[2,2,4,384]{3,2,1,0:T(4,128)S(1)} %get-tuple-element.176, f32[2,2,4,128]{3,2,1,0:T(4,128)S(1)} %get-tuple-element.405, f32[2,2,4,384]{3,2,1,0:T(4,128)S(1)} %fusion.298, ...), kind=kLoop, calls=%fused_computation.248 | loop fusion | flops 33024000 | bytes 312832 | tf_op jit(solution)/shard_map/reduce_sum | solution.py:98
  286.5 7.1 %multiply_reduce_fusion.4 = (f32[2,2,4,128]{3,2,1,0:T(4,128)S(1)}, f32[2,2,4,128]{3,2,1,0:T(4,128)S(1)}, f32[2,2,4,128]{3,2,1,0:T(4,128)S(1)}) fusion(f32[2,2,4,384]{3,2,1,0:T(4,128)S(1)} %get-tuple-element.182, f32[2,2,4,128]{3,2,1,0:T(4,128)S(1)} %get-tuple-element.405, f32[2,2,4,384]{3,2,1,0:T(4,128)S(1)} %get-tuple-element.472, ...), kind=kLoop, calls=%fused_computation.243 | loop fusion | flops 32237568 | bytes 312832 | tf_op jit(solution)/shard_map/reduce_sum | solution.py:98
  293.6 7.2 %multiply_reduce_fusion.2 = (f32[2,2,4,128]{3,2,1,0:T(4,128)S(1)}, f32[2,2,4,128]{3,2,1,0:T(4,128)S(1)}, f32[2,2,4,128]{3,2,1,0:T(4,128)S(1)}) fusion(f32[2,2,4,384]{3,2,1,0:T(4,128)S(1)} %get-tuple-element.188, f32[2,2,4,128]{3,2,1,0:T(4,128)S(1)} %get-tuple-element.405, f32[2,2,4,384]{3,2,1,0:T(4,128)S(1)} %fusion.299, ...), kind=kLoop, calls=%fused_computation.238 | loop fusion | flops 33024000 | bytes 312832 | tf_op jit(solution)/shard_map/reduce_sum | solution.py:98
  (275 shorter events, 51.4 us)
Async XLA Ops:
  0.6 27.6 %copy-start.9 = (f32[3]{0:T(128)S(1)}, f32[3]{0:T(128)}, u32[]{:S(2)}) copy-start(f32[3]{0:T(128)} %constant.128) | copy-start | bytes 40
  0.6 27.4 %copy-start.4 = (f32[3,2,2,4,128]{4,3,2,1,0:T(4,128)S(1)}, f32[3,2,2,4,128]{4,3,2,1,0:T(4,128)}, u32[]{:S(2)}) copy-start(f32[3,2,2,4,128]{4,3,2,1,0:T(4,128)} %param.9) | copy-start | bytes 73732
  0.7 27.4 %copy-start.5 = (f32[3,2,2,4,128]{4,3,2,1,0:T(4,128)S(1)}, f32[3,2,2,4,128]{4,3,2,1,0:T(4,128)}, u32[]{:S(2)}) copy-start(f32[3,2,2,4,128]{4,3,2,1,0:T(4,128)} %param.10) | copy-start | bytes 73732
  0.7 17.3 %copy-start.8 = (s32[2,2,4]{2,1,0:T(2,128)S(1)}, s32[2,2,4]{2,1,0:T(2,128)}, u32[]{:S(2)}) copy-start(s32[2,2,4]{2,1,0:T(2,128)} %param.11) | copy-start | bytes 196
  2.2 35.9 %collective-permute-start.4 = (f32[6,1,2,4,128]{4,3,2,1,0:T(4,128)S(1)}, f32[6,1,2,4,128]{4,3,2,1,0:T(4,128)S(1)}, u32[]{:S(2)}, u32[]{:S(2)}) collective-permute-start(f32[6,1,2,4,128]{4,3,2,1,0:T(4,128)S(1)} %get-tuple-element.415), channel_id=1, source_target_pairs={{0,4},{4,8},{8,12},{12,16},{16,20},{20,24},{24,28},{28,32},{32,36}... | collective-permute-start | bytes 73736 | tf_op jit(solution)/shard_map/ppermute | solution.py:30
  5.6 32.5 %collective-permute-start.5 = (f32[6,1,2,4,128]{4,3,2,1,0:T(4,128)S(1)}, f32[6,1,2,4,128]{4,3,2,1,0:T(4,128)S(1)}, u32[]{:S(2)}, u32[]{:S(2)}) collective-permute-start(f32[6,1,2,4,128]{4,3,2,1,0:T(4,128)S(1)} %get-tuple-element.416), channel_id=1, source_target_pairs={{4,0},{8,4},{12,8},{16,12},{20,16},{24,20},{28,24},{32,28},{36,32}... | collective-permute-start | bytes 73736 | tf_op jit(solution)/shard_map/ppermute | solution.py:32
  18.0 10.3 %collective-permute-start = (f32[1,1,2,4,1]{3,2,1,4,0:T(2,128)S(1)}, f32[1,1,2,4,1]{3,2,1,4,0:T(2,128)S(1)}, u32[]{:S(2)}, u32[]{:S(2)}) collective-permute-start(f32[1,1,2,4,1]{3,2,1,4,0:T(2,128)S(1)} %get-tuple-element.484), channel_id=1, source_target_pairs={{0,4},{4,8},{8,12},{12,16},{16,20},{20,24},{24,28},{28,32},{32,36}... | collective-permute-start | bytes 104 | tf_op jit(solution)/shard_map/ppermute | solution.py:30
  19.9 9.4 %collective-permute-start.1 = (f32[1,1,2,4,1]{3,2,1,4,0:T(2,128)S(1)}, f32[1,1,2,4,1]{3,2,1,4,0:T(2,128)S(1)}, u32[]{:S(2)}, u32[]{:S(2)}) collective-permute-start(f32[1,1,2,4,1]{3,2,1,4,0:T(2,128)S(1)} %get-tuple-element.485), channel_id=1, source_target_pairs={{4,0},{8,4},{12,8},{16,12},{20,16},{24,20},{28,24},{32,28},{36,32}... | collective-permute-start | bytes 104 | tf_op jit(solution)/shard_map/ppermute | solution.py:32
  29.3 7.1 %collective-permute-start.2 = (f32[1,4,1,4,1]{3,2,1,4,0:T(1,128)S(1)}, f32[1,4,1,4,1]{3,2,1,4,0:T(1,128)S(1)}, u32[]{:S(2)}, u32[]{:S(2)}) collective-permute-start(f32[1,4,1,4,1]{3,2,1,4,0:T(1,128)S(1)} %get-tuple-element.480), channel_id=1, source_target_pairs={{0,1},{1,2},{2,3},{4,5},{5,6},{6,7},{8,9},{9,10},{10,11},{12,13},{... | collective-permute-start | bytes 200 | tf_op jit(solution)/shard_map/ppermute | solution.py:30
  31.2 6.4 %collective-permute-start.3 = (f32[1,4,1,4,1]{3,2,1,4,0:T(1,128)S(1)}, f32[1,4,1,4,1]{3,2,1,4,0:T(1,128)S(1)}, u32[]{:S(2)}, u32[]{:S(2)}) collective-permute-start(f32[1,4,1,4,1]{3,2,1,4,0:T(1,128)S(1)} %get-tuple-element.481), channel_id=1, source_target_pairs={{1,0},{2,1},{3,2},{5,4},{6,5},{7,6},{9,8},{10,9},{11,10},{13,12},{... | collective-permute-start | bytes 200 | tf_op jit(solution)/shard_map/ppermute | solution.py:32
  38.1 7.1 %collective-permute-start.6 = (f32[6,4,1,4,128]{4,3,2,1,0:T(4,128)S(1)}, f32[6,4,1,4,128]{4,3,2,1,0:T(4,128)S(1)}, u32[]{:S(2)}, u32[]{:S(2)}) collective-permute-start(f32[6,4,1,4,128]{4,3,2,1,0:T(4,128)S(1)} %get-tuple-element.303), channel_id=1, source_target_pairs={{0,1},{1,2},{2,3},{4,5},{5,6},{6,7},{8,9},{9,10},{10,11},{12,13},{... | collective-permute-start | bytes 147464 | tf_op jit(solution)/shard_map/ppermute | solution.py:30
  40.1 6.9 %collective-permute-start.7 = (f32[6,4,1,4,128]{4,3,2,1,0:T(4,128)S(1)}, f32[6,4,1,4,128]{4,3,2,1,0:T(4,128)S(1)}, u32[]{:S(2)}, u32[]{:S(2)}) collective-permute-start(f32[6,4,1,4,128]{4,3,2,1,0:T(4,128)S(1)} %get-tuple-element.304), channel_id=1, source_target_pairs={{1,0},{2,1},{3,2},{5,4},{6,5},{7,6},{9,8},{10,9},{11,10},{13,12},{... | collective-permute-start | bytes 147464 | tf_op jit(solution)/shard_map/ppermute | solution.py:32
  47.0 0.7 copy-start.3
  47.8 0.9 slice-start.2
  78.1 10.9 %collective-permute-start.8 = (f32[1,1,2,4,128]{4,3,2,1,0:T(4,128)S(1)}, f32[1,1,2,4,128]{4,3,2,1,0:T(4,128)S(1)}, u32[]{:S(2)}, u32[]{:S(2)}) collective-permute-start(f32[1,1,2,4,128]{4,3,2,1,0:T(4,128)S(1)} %get-tuple-element.478), channel_id=1, source_target_pairs={{0,4},{4,8},{8,12},{12,16},{16,20},{20,24},{24,28},{28,32},{32,36}... | collective-permute-start | bytes 12296 | tf_op jit(solution)/shard_map/ppermute | solution.py:30
  80.0 9.7 %collective-permute-start.9 = (f32[1,1,2,4,128]{4,3,2,1,0:T(4,128)S(1)}, f32[1,1,2,4,128]{4,3,2,1,0:T(4,128)S(1)}, u32[]{:S(2)}, u32[]{:S(2)}) collective-permute-start(f32[1,1,2,4,128]{4,3,2,1,0:T(4,128)S(1)} %get-tuple-element.479), channel_id=1, source_target_pairs={{4,0},{8,4},{12,8},{16,12},{20,16},{24,20},{28,24},{32,28},{36,32}... | collective-permute-start | bytes 12296 | tf_op jit(solution)/shard_map/ppermute | solution.py:32
  89.7 7.3 %collective-permute-start.10 = (f32[1,4,1,4,128]{4,3,2,1,0:T(4,128)S(1)}, f32[1,4,1,4,128]{4,3,2,1,0:T(4,128)S(1)}, u32[]{:S(2)}, u32[]{:S(2)}) collective-permute-start(f32[1,4,1,4,128]{4,3,2,1,0:T(4,128)S(1)} %get-tuple-element.468), channel_id=1, source_target_pairs={{0,1},{1,2},{2,3},{4,5},{5,6},{6,7},{8,9},{9,10},{10,11},{12,13},{... | collective-permute-start | bytes 24584 | tf_op jit(solution)/shard_map/ppermute | solution.py:30
  91.7 6.5 %collective-permute-start.11 = (f32[1,4,1,4,128]{4,3,2,1,0:T(4,128)S(1)}, f32[1,4,1,4,128]{4,3,2,1,0:T(4,128)S(1)}, u32[]{:S(2)}, u32[]{:S(2)}) collective-permute-start(f32[1,4,1,4,128]{4,3,2,1,0:T(4,128)S(1)} %get-tuple-element.469), channel_id=1, source_target_pairs={{1,0},{2,1},{3,2},{5,4},{6,5},{7,6},{9,8},{10,9},{11,10},{13,12},{... | collective-permute-start | bytes 24584 | tf_op jit(solution)/shard_map/ppermute | solution.py:32
  155.6 7.2 %copy-start.7 = (f32[3]{0:T(128)S(1)}, f32[3]{0:T(128)}, u32[]{:S(2)}) copy-start(f32[3]{0:T(128)} %constant.129) | copy-start | bytes 40
  163.0 22.6 %copy-start = (f32[6,2,2,4,128]{4,3,2,1,0:T(4,128)}, f32[6,2,2,4,128]{4,3,2,1,0:T(4,128)S(1)}, u32[]{:S(2)}) copy-start(f32[6,2,2,4,128]{4,3,2,1,0:T(4,128)S(1)} %fusion.181) | copy-start | bytes 147460
  163.0 10.3 %collective-permute-start.12 = (f32[6,1,2,4,128]{4,3,2,1,0:T(4,128)S(1)}, f32[6,1,2,4,128]{4,3,2,1,0:T(4,128)S(1)}, u32[]{:S(2)}, u32[]{:S(2)}) collective-permute-start(f32[6,1,2,4,128]{4,3,2,1,0:T(4,128)S(1)} %get-tuple-element.408), channel_id=1, source_target_pairs={{0,4},{4,8},{8,12},{12,16},{16,20},{20,24},{24,28},{28,32},{32,36}... | collective-permute-start | bytes 73736 | tf_op jit(solution)/shard_map/ppermute | solution.py:30
  165.0 9.9 %collective-permute-start.13 = (f32[6,1,2,4,128]{4,3,2,1,0:T(4,128)S(1)}, f32[6,1,2,4,128]{4,3,2,1,0:T(4,128)S(1)}, u32[]{:S(2)}, u32[]{:S(2)}) collective-permute-start(f32[6,1,2,4,128]{4,3,2,1,0:T(4,128)S(1)} %get-tuple-element.409), channel_id=1, source_target_pairs={{4,0},{8,4},{12,8},{16,12},{20,16},{24,20},{28,24},{32,28},{36,32}... | collective-permute-start | bytes 73736 | tf_op jit(solution)/shard_map/ppermute | solution.py:32
  174.9 7.3 %collective-permute-start.14 = (f32[6,4,1,4,128]{4,3,2,1,0:T(4,128)S(1)}, f32[6,4,1,4,128]{4,3,2,1,0:T(4,128)S(1)}, u32[]{:S(2)}, u32[]{:S(2)}) collective-permute-start(f32[6,4,1,4,128]{4,3,2,1,0:T(4,128)S(1)} %get-tuple-element.281), channel_id=1, source_target_pairs={{0,1},{1,2},{2,3},{4,5},{5,6},{6,7},{8,9},{9,10},{10,11},{12,13},{... | collective-permute-start | bytes 147464 | tf_op jit(solution)/shard_map/ppermute | solution.py:30
  176.9 6.9 %collective-permute-start.15 = (f32[6,4,1,4,128]{4,3,2,1,0:T(4,128)S(1)}, f32[6,4,1,4,128]{4,3,2,1,0:T(4,128)S(1)}, u32[]{:S(2)}, u32[]{:S(2)}) collective-permute-start(f32[6,4,1,4,128]{4,3,2,1,0:T(4,128)S(1)} %get-tuple-element.282), channel_id=1, source_target_pairs={{1,0},{2,1},{3,2},{5,4},{6,5},{7,6},{9,8},{10,9},{11,10},{13,12},{... | collective-permute-start | bytes 147464 | tf_op jit(solution)/shard_map/ppermute | solution.py:32
  184.6 0.9 slice-start.1
  185.7 0.7 slice-start
  215.5 19.5 %copy-start.6 = (f32[2,2,4,128]{3,2,1,0:T(4,128)}, f32[2,2,4,128]{3,2,1,0:T(4,128)S(1)}, u32[]{:S(2)}) copy-start(f32[2,2,4,128]{3,2,1,0:T(4,128)S(1)} %get-tuple-element.82) | copy-start | bytes 24580
  215.6 11.7 %collective-permute-start.16 = (f32[1,1,2,4,128]{4,3,2,1,0:T(4,128)S(1)}, f32[1,1,2,4,128]{4,3,2,1,0:T(4,128)S(1)}, u32[]{:S(2)}, u32[]{:S(2)}) collective-permute-start(f32[1,1,2,4,128]{4,3,2,1,0:T(4,128)S(1)} %get-tuple-element.473), channel_id=1, source_target_pairs={{0,4},{4,8},{8,12},{12,16},{16,20},{20,24},{24,28},{28,32},{32,36}... | collective-permute-start | bytes 12296 | tf_op jit(solution)/shard_map/ppermute | solution.py:30
  217.5 9.8 %collective-permute-start.17 = (f32[1,1,2,4,128]{4,3,2,1,0:T(4,128)S(1)}, f32[1,1,2,4,128]{4,3,2,1,0:T(4,128)S(1)}, u32[]{:S(2)}, u32[]{:S(2)}) collective-permute-start(f32[1,1,2,4,128]{4,3,2,1,0:T(4,128)S(1)} %get-tuple-element.474), channel_id=1, source_target_pairs={{4,0},{8,4},{12,8},{16,12},{20,16},{24,20},{28,24},{32,28},{36,32}... | collective-permute-start | bytes 12296 | tf_op jit(solution)/shard_map/ppermute | solution.py:32
  226.0 0.8 copy-start.1
  227.3 7.7 %collective-permute-start.18 = (f32[1,4,1,4,128]{4,3,2,1,0:T(4,128)S(1)}, f32[1,4,1,4,128]{4,3,2,1,0:T(4,128)S(1)}, u32[]{:S(2)}, u32[]{:S(2)}) collective-permute-start(f32[1,4,1,4,128]{4,3,2,1,0:T(4,128)S(1)} %get-tuple-element.464), channel_id=1, source_target_pairs={{0,1},{1,2},{2,3},{4,5},{5,6},{6,7},{8,9},{9,10},{10,11},{12,13},{... | collective-permute-start | bytes 24584 | tf_op jit(solution)/shard_map/ppermute | solution.py:30
  229.3 6.9 %collective-permute-start.19 = (f32[1,4,1,4,128]{4,3,2,1,0:T(4,128)S(1)}, f32[1,4,1,4,128]{4,3,2,1,0:T(4,128)S(1)}, u32[]{:S(2)}, u32[]{:S(2)}) collective-permute-start(f32[1,4,1,4,128]{4,3,2,1,0:T(4,128)S(1)} %get-tuple-element.465), channel_id=1, source_target_pairs={{1,0},{2,1},{3,2},{5,4},{6,5},{7,6},{9,8},{10,9},{11,10},{13,12},{... | collective-permute-start | bytes 24584 | tf_op jit(solution)/shard_map/ppermute | solution.py:32
  (1 other events, 0.7 us)
where the time goes:
time: 305 us; the launch traced here: 302 us
  other arithmetic  188 us (62%)
  starting transfers between devices  93.1 us (31%)
  waiting for transfers between devices  9.93 us (3%)
  local copies, waits for them, and re-layouts  7.72 us (3%)
    reduce_sum x18, other arithmetic, force_terms(): jnp.sum(strength * separation[axis_num], axis=-1)  128 us
    ppermute x10, starting transfers between devices, with_halo(): lax.ppermute(head, axis, [((i + 1) % count, i) for i in range(ends)])  72.4 us
    reduce_sum x6, other arithmetic, density_terms(): return particle_mass * jnp.sum(weight * source_live[..., None, :], axis=-1)  57.7 us
    ppermute x10, starting transfers between devices, with_halo(): lax.ppermute(tail, axis, [(i, (i + 1) % count) for i in range(ends)])  20.7 us
    ppermute x10, waiting for transfers between devices, with_halo(): lax.ppermute(head, axis, [((i + 1) % count, i) for i in range(ends)])  9.9 us
  transfers between devices with their start and end apart: 20, of which 8 were waited for; matrix products, arithmetic and copies ran while one was open for 0% of the time, Pallas kernels for 0%

commit v1 on v0

v1 whole, which is shorter than its diff:
```python
import functools
import math

import jax
import jax.numpy as jnp
from jax import lax
from jax.experimental import pallas as pl
from jax.experimental.pallas import tpu as pltpu
from jax.sharding import PartitionSpec as P

STEPS = 2
SLOTS = 128
MASS = 8.0 / SLOTS
KERNEL_NORM = 21.0 / (16.0 * math.pi)
TAIT = 10.0 * 10.0 / 7.0
TIME_STEP = 0.02
GRAVITY = 1.0
FAR = 1000.0
TINY = 1e-30

PARTS_J = (0, 0, 1, 1, 0, 2)
PARTS_I = (0, 1, 0, 1, 2, 0)
ROW_X = 0
ROW_NJ = 18
ROW_ONE = 21
ROW_V = 24
ROW_WJ = 42
ROW_RHO = 45
ROW_P = 48
DEPTH = 128


def split3(value):
    high = value.astype(jnp.bfloat16).astype(jnp.float32)
    rest = value - high
    middle = rest.astype(jnp.bfloat16).astype(jnp.float32)
    return (high, middle, rest - middle)


def cell_z(rows):
    return lax.broadcasted_iota(jnp.int32, (rows, SLOTS), 0).astype(jnp.float32)


def dot(lhs, rhs):
    return jnp.dot(lhs, rhs, preferred_element_type=jnp.float32)


def fold(tile):
    return jnp.sum(tile.reshape(tile.shape[0] // 8, 8, tile.shape[1]), axis=0)


def column_of(refs, comp, ix, iy):
    own, left, right, down, up = refs
    if iy == 0:
        return down[comp, ix]
    if iy == 3:
        return up[comp, ix]
    if ix < 2:
        return left[comp, ix, iy - 1]
    if ix < 4:
        return own[comp, ix - 2, iy - 1]
    return right[comp, ix - 4, iy - 1]


def centred(refs, ix, iy):
    shifts = (ix - 3.0, iy - 2.0, None)
    places = []
    for axis in range(3):
        half = 0.5 * column_of(refs, axis, ix, iy)
        shift = shifts[axis] if axis < 2 else cell_z(half.shape[0]) - 0.5 * half.shape[0]
        places.append(half + shift)
    return places


def source_rows(refs, ix, iy, with_velocity):
    live = column_of(refs, 6, ix, iy) > 0.5
    places = [jnp.where(live, place, FAR) for place in centred(refs, ix, iy)]
    rows = {}
    for axis in range(3):
        parts = split3(places[axis])
        for at, part in enumerate(PARTS_J):
            rows[ROW_X + 6 * axis + at] = parts[part]
    norm = places[0] * places[0] + places[1] * places[1] + places[2] * places[2]
    for at, part in enumerate(split3(norm)):
        rows[ROW_NJ + at] = part
        rows[ROW_ONE + at] = jnp.ones_like(part)
    if with_velocity:
        speeds = [column_of(refs, 3 + axis, ix, iy) for axis in range(3)]
        along = 0.0
        for axis in range(3):
            parts = split3(speeds[axis])
            for at, part in enumerate(PARTS_J):
                rows[ROW_V + 6 * axis + at] = parts[part]
            along = along + speeds[axis] * places[axis]
        for at, part in enumerate(split3(along)):
            rows[ROW_WJ + at] = part
    return rows


def put_rows(table, column, rows):
    for row, value in rows.items():
        table[column, :, row, :] = value


def turn_tables(table, turned, columns, cells_z):
    def body(step, carry):
        column, z = step // cells_z, step % cells_z
        turned[column, z] = jnp.transpose(table[column, z]).astype(jnp.bfloat16)
        return carry

    lax.fori_loop(0, columns * cells_z, body, 0)


def density_kernel(own, left, right, down, up, rho_ref, table, turned, weights):
    refs = (own, left, right, down, up)
    cells_z = own.shape[3]
    table[...] = jnp.zeros_like(table)
    weights[...] = jnp.zeros_like(weights)
    for ix in range(6):
        for iy in range(4):
            put_rows(table, ix * 4 + iy, source_rows(refs, ix, iy, False))
    turn_tables(table, turned, 24, cells_z)
    for tx in range(4):
        for ty in range(2):
            places = centred(refs, tx + 1, ty + 1)
            rows = {}
            for axis in range(3):
                parts = split3(-2.0 * places[axis])
                for at, part in enumerate(PARTS_I):
                    rows[ROW_X + 6 * axis + at] = parts[part]
            norm = places[0] * places[0] + places[1] * places[1] + places[2] * places[2]
            for at, part in enumerate(split3(norm)):
                rows[ROW_NJ + at] = jnp.ones_like(part)
                rows[ROW_ONE + at] = part
            put_rows(weights, tx * 2 + ty, rows)

    def target(step, carry):
        tx, ty = step // 2, step % 2
        rhs = [
            jnp.concatenate(
                [weights[step, 2 * pair].astype(jnp.bfloat16), weights[step, 2 * pair + 1].astype(jnp.bfloat16)], axis=1
            )
            for pair in range(cells_z // 2)
        ]

        def source(dx, sums):
            sums = list(sums)
            for dy in range(3):
                column = (tx + dx) * 4 + ty + dy
                for pair in range(cells_z // 2):
                    for z in range(max(0, 2 * pair - 1), min(cells_z, 2 * pair + 3)):
                        gap = dot(turned[column, z], rhs[pair])
                        for half in range(2):
                            zt = 2 * pair + half
                            if abs(zt - z) > 1:
                                continue
                            near = jnp.maximum(gap[:, half * SLOTS : (half + 1) * SLOTS], TINY)
                            inside = jnp.maximum(1.0 - near * lax.rsqrt(near), 0.0)
                            square = inside * inside
                            fourth = square * square
                            sums[2 * zt] = sums[2 * zt] + fold(fourth)
                            sums[2 * zt + 1] = sums[2 * zt + 1] + fold(fourth * inside)
            return tuple(sums)

        zero = jnp.zeros((8, SLOTS), jnp.float32)
        sums = lax.fori_loop(0, 3, source, (zero,) * (2 * cells_z))
        for zt in range(cells_z):
            total = 5.0 * sums[2 * zt] - 4.0 * sums[2 * zt + 1]
            rho_ref[tx, ty, pl.ds(zt, 1), :] = (MASS * KERNEL_NORM) * jnp.sum(total, axis=0, keepdims=True)
        return carry

    lax.fori_loop(0, 8, target, 0)
    for ix in range(2):
        for iy in range(2):
            rho_ref[ix + 1, iy] = rho_ref[ix + 1, iy] + (1.0 - own[6, ix, iy]) * (MASS * KERNEL_NORM)


def pressure_ratio(density):
    cubed = density * density * density
    return TAIT * (cubed * cubed * density - 1.0) / (density * density)


def force_kernel(own, left, right, down, up, rho, rho_down, rho_up, out_ref, table, turned, weights, spread, rows_i):
    refs = (own, left, right, down, up)
    cells_z = own.shape[3]
    table[...] = jnp.zeros_like(table)
    weights[...] = jnp.zeros_like(weights)
    for ix in range(4):
        for iy in range(4):
            rows = source_rows(refs, ix + 1, iy, True)
            density = rho_down[ix] if iy == 0 else rho_up[ix] if iy == 3 else rho[ix, iy - 1]
            density = jnp.maximum(density, MASS * KERNEL_NORM)
            for at, part in enumerate(split3(density)):
                rows[ROW_RHO + at] = part
            for at, part in enumerate(split3(pressure_ratio(density))):
                rows[ROW_P + at] = part
            put_rows(table, ix * 4 + iy, rows)
    turn_tables(table, turned, 16, cells_z)

    at_row = lax.broadcasted_iota(jnp.int32, (DEPTH, SLOTS), 0)
    picks = []
    for rows in (
        tuple(range(ROW_RHO, ROW_RHO + 3)),
        tuple(range(ROW_P, ROW_P + 3)),
        (ROW_X, ROW_X + 2, ROW_X + 5),
        (ROW_X + 6, ROW_X + 8, ROW_X + 11),
        (ROW_X + 12, ROW_X + 14, ROW_X + 17),
    ):
        chosen = (at_row == rows[0]) | (at_row == rows[1]) | (at_row == rows[2])
        picks.append(jnp.where(chosen, 1.0, 0.0).astype(jnp.bfloat16))

    def spread_cell(step, carry):
        column, z = step // cells_z, step % cells_z
        for at, pick in enumerate(picks):
            spread[column, z, at] = dot(turned[column, z], pick)
        return carry

    lax.fori_loop(0, 16 * cells_z, spread_cell, 0)

    for tx in range(2):
        for ty in range(2):
            places = centred(refs, tx + 2, ty + 1)
            speeds = [column_of(refs, 3 + axis, tx + 2, ty + 1) for axis in range(3)]
            gap_rows, near_rows = {}, {}
            norm, along = 0.0, 0.0
            for axis in range(3):
                gap_parts = split3(-2.0 * places[axis])
                place_parts = split3(2.0 * places[axis])
                speed_parts = split3(2.0 * speeds[axis])
                for at, part in enumerate(PARTS_I):
                    gap_rows[ROW_X + 6 * axis + at] = gap_parts[part]
                    near_rows[ROW_X + 6 * axis + at] = speed_parts[part]
                    near_rows[ROW_V + 6 * axis + at] = place_parts[part]
                norm = norm + places[axis] * places[axis]
                along = along + places[axis] * speeds[axis]
            for at, (part, other) in enumerate(zip(split3(norm), split3(-2.0 * along))):
                gap_rows[ROW_NJ + at] = jnp.ones_like(part)
                gap_rows[ROW_ONE + at] = part
                near_rows[ROW_WJ + at] = jnp.full_like(part, -2.0)
                near_rows[ROW_ONE + at] = other
            put_rows(weights.at[0], tx * 2 + ty, gap_rows)
            put_rows(weights.at[1], tx * 2 + ty, near_rows)
            density = jnp.maximum(rho[tx + 1, ty], MASS * KERNEL_NORM)
            rows_i[tx * 2 + ty, 0] = density
            rows_i[tx * 2 + ty, 1] = pressure_ratio(density)
            for axis in range(3):
                rows_i[tx * 2 + ty, 2 + axis] = places[axis]

    def target(step, carry):
        tx, ty = step // 2, step % 2
        rhs = [
            jnp.concatenate([weights[0, step, z].astype(jnp.bfloat16), weights[1, step, z].astype(jnp.bfloat16)], axis=1)
            for z in range(cells_z)
        ]
        rho_i = [rows_i[step, 0, pl.ds(z, 1), :] for z in range(cells_z)]
        ratio_i = [rows_i[step, 1, pl.ds(z, 1), :] for z in range(cells_z)]

        def source(dx, sums):
            sums = list(sums)
            for dy in range(3):
                column = (tx + dx) * 4 + ty + dy
                for zt in range(cells_z):
                    for z in range(max(0, zt - 1), min(cells_z, zt + 2)):
                        both = dot(turned[column, z], rhs[zt])
                        near = jnp.maximum(both[:, :SLOTS], TINY)
                        inside = jnp.maximum(1.0 - near * lax.rsqrt(near), 0.0)
                        closing = jnp.maximum(both[:, SLOTS:], 0.0)
                        below = (near + 0.0025) * (spread[column, z, 0] + rho_i[zt])
                        strength = (spread[column, z, 1] + ratio_i[zt]) + closing / below
                        strength = strength * (inside * inside * inside)
                        sums[4 * zt] = sums[4 * zt] + fold(strength)
                        for axis in range(3):
                            sums[4 * zt + 1 + axis] = sums[4 * zt + 1 + axis] + fold(strength * spread[column, z, 2 + axis])
            return tuple(sums)

        zero = jnp.zeros((8, SLOTS), jnp.float32)
        sums = lax.fori_loop(0, 3, source, (zero,) * (4 * cells_z))
        for zt in range(cells_z):
            row = pl.ds(zt, 1)
            whole = jnp.sum(sums[4 * zt], axis=0, keepdims=True)
            live = own[6, tx, ty, row, :] > 0.5
            for axis in range(3):
                part = jnp.sum(sums[4 * zt + 1 + axis], axis=0, keepdims=True)
                pull = (10.0 * KERNEL_NORM * MASS) * (rows_i[step, 2 + axis, row, :] * whole - part)
                if axis == 2:
                    pull = pull - GRAVITY
                old_place = own[axis, tx, ty, row, :]
                old_speed = own[3 + axis, tx, ty, row, :]
                speed = old_speed + TIME_STEP * pull
                out_ref[axis, tx, ty, row, :] = jnp.where(live, old_place + TIME_STEP * speed, old_place)
                out_ref[3 + axis, tx, ty, row, :] = jnp.where(live, speed, old_speed)
            out_ref[6, tx, ty, row, :] = own[6, tx, ty, row, :]
        return carry

    lax.fori_loop(0, 4, target, 0)


VMEM_SPEC = pl.BlockSpec(memory_space=pltpu.VMEM)


def densities(state, left, right, down, up):
    cells_z = state.shape[3]
    return pl.pallas_call(
        density_kernel,
        name="density",
        out_shape=jax.ShapeDtypeStruct((4, 2, cells_z, SLOTS), jnp.float32),
        in_specs=[VMEM_SPEC] * 5,
        out_specs=VMEM_SPEC,
        scratch_shapes=[
            pltpu.VMEM((24, cells_z, DEPTH, SLOTS), jnp.float32),
            pltpu.VMEM((24, cells_z, SLOTS, DEPTH), jnp.bfloat16),
            pltpu.VMEM((8, cells_z, DEPTH, SLOTS), jnp.float32),
        ],
        compiler_params=pltpu.CompilerParams(vmem_limit_bytes=48 << 20),
    )(state, left, right, down, up)


def moved(state, left, right, down, up, rho, rho_down, rho_up):
    cells_z = state.shape[3]
    return pl.pallas_call(
        force_kernel,
        name="force",
        out_shape=jax.ShapeDtypeStruct(state.shape, jnp.float32),
        in_specs=[VMEM_SPEC] * 8,
        out_specs=VMEM_SPEC,
        scratch_shapes=[
            pltpu.VMEM((16, cells_z, DEPTH, SLOTS), jnp.float32),
            pltpu.VMEM((16, cells_z, SLOTS, DEPTH), jnp.bfloat16),
            pltpu.VMEM((2, 4, cells_z, DEPTH, SLOTS), jnp.float32),
            pltpu.VMEM((16, cells_z, 5, SLOTS, SLOTS), jnp.float32),
            pltpu.VMEM((4, 5, cells_z, SLOTS), jnp.float32),
        ],
        compiler_params=pltpu.CompilerParams(vmem_limit_bytes=56 << 20),
    )(state, left, right, down, up, rho, rho_down, rho_up)


def from_below(value, axis):
    count = lax.axis_size(axis)
    return lax.ppermute(value, axis, [(i, i + 1) for i in range(count - 1)])


def from_above(value, axis):
    count = lax.axis_size(axis)
    return lax.ppermute(value, axis, [(i + 1, i) for i in range(count - 1)])


def per_device(offsets, velocity, occupancy):
    slot_rank = jnp.arange(SLOTS, dtype=jnp.int32)
    live = (slot_rank < occupancy[..., None]).astype(jnp.float32)
    state = jnp.concatenate([offsets, velocity, live[None]], axis=0)
    rho = None
    for _ in range(STEPS):
        left, right = from_below(state, "slab"), from_above(state, "slab")
        edge = lambda y: jnp.concatenate([left[:, :, y], state[:, :, y], right[:, :, y]], axis=1)
        down, up = from_below(edge(1), "col"), from_above(edge(0), "col")
        rho = densities(state, left, right, down, up)
        rho_down, rho_up = from_below(rho[:, 1], "col"), from_above(rho[:, 0], "col")
        state = moved(state, left, right, down, up, rho, rho_down, rho_up)
    return (state[0:3], state[3:6], rho[1:3])


def solution(mesh):
    placed = P(None, "slab", "col", None, None)
    return jax.shard_map(
        per_device,
        mesh=mesh,
        in_specs=(placed, placed, P("slab", "col", None)),
        out_specs=(placed, placed, P("slab", "col", None, None)),
        check_vma=False,
    )
```

time: 305 us -> 226 us (0.74)
  other arithmetic: 188 us -> 0.93 us
  Pallas kernels: 0 us -> 148 us
  starting transfers between devices: 93.1 us -> 54.3 us
    reduce_sum x24 -> x0, other arithmetic: 185 us -> none  [the longest x18 128 us: force_terms(): jnp.sum(strength * separation[axis_num], axis=-1)]
    pallas_call x0 -> x4, Pallas kernels: none -> 148 us  [the longest x2 83.7 us: moved(): pl.pallas_call(force_kernel, name='force', out_shape=jax.ShapeDtypeStruct...]
    ppermute x20 -> x12, starting transfers between devices: 93.1 us -> 54.3 us  [the longest x6 41.3 us: from_above(): return lax.ppermute(value, axis, [(i + 1, i) for i in range(count - 1)])]
    ppermute x20 -> x12, waiting for transfers between devices: 9.93 us -> 12.7 us  [the longest x6 6.98 us: from_above(): return lax.ppermute(value, axis, [(i + 1, i) for i in range(count - 1)])]
  transfers between devices with their start and end apart: 20 -> 12, of which waited for: 8 -> 10; matrix products, arithmetic and copies ran while one was open for 0% -> 0% of each run, Pallas kernels for 0% -> 0%
where the time goes in v1:
time: 226 us; the launch traced here: 223 us
  Pallas kernels  148 us (65%)
  starting transfers between devices  54.3 us (24%)
  waiting for transfers between devices  12.7 us (6%)
  local copies, waits for them, and re-layouts  5.55 us (2%)
    pallas_call x2, Pallas kernels, moved(): pl.pallas_call(force_kernel, name='force', out_shape=jax.ShapeDtypeStruct...  83.7 us
    pallas_call x2, Pallas kernels, densities(): pl.pallas_call(density_kernel, name='density', out_shape=jax.ShapeDtypeSt...  64.6 us
    ppermute x6, starting transfers between devices, from_above(): return lax.ppermute(value, axis, [(i + 1, i) for i in range(count - 1)])  41.3 us
    ppermute x6, starting transfers between devices, from_below(): return lax.ppermute(value, axis, [(i, i + 1) for i in range(count - 1)])  13 us
    ppermute x6, waiting for transfers between devices, from_above(): return lax.ppermute(value, axis, [(i + 1, i) for i in range(count - 1)])  6.98 us
    ppermute x6, waiting for transfers between devices, from_below(): return lax.ppermute(value, axis, [(i, i + 1) for i in range(count - 1)])  5.75 us
  transfers between devices with their start and end apart: 12, of which 10 were waited for; matrix products, arithmetic and copies ran while one was open for 0% of the time, Pallas kernels for 0%

profile of v1, /device:TPU:24, one launch (start us, length us, event | category | flops | bytes accessed | tf_op | source)
XLA Modules:
  0.0 222.8 jit_solution(956037716805463453)
XLA Ops:
  0.6 0.7 copy.6
  1.4 0.8 pad_maximum_fusion.4
  2.2 3.4 %collective-permute-start = (f32[7,2,2,4,128]{4,3,1,0,2:T(4,128)S(1)}, f32[7,2,2,4,128]{4,3,1,0,2:T(4,128)S(1)}, u32[]{:S(2)}, u32[]{:S(2)}) collective-permute-start(f32[7,2,2,4,128]{4,3,1,0,2:T(4,128)S(1)} %pad_maximum_fusion.4), channel_id=1, source_target_pairs={{0,4},{4,8},{8,12},{12,16},{16,20},{20,24},{24,28},{28,32},{32,36}... | collective-permute-start | bytes 172040 | tf_op jit(solution)/shard_map/ppermute | solution.py:339
  5.6 12.3 %collective-permute-start.1 = (f32[7,2,2,4,128]{4,3,1,0,2:T(4,128)S(1)}, f32[7,2,2,4,128]{4,3,1,0,2:T(4,128)S(1)}, u32[]{:S(2)}, u32[]{:S(2)}) collective-permute-start(f32[7,2,2,4,128]{4,3,1,0,2:T(4,128)S(1)} %pad_maximum_fusion.4), channel_id=1, source_target_pairs={{4,0},{8,4},{12,8},{16,12},{20,16},{24,20},{28,24},{32,28},{36,32}... | collective-permute-start | bytes 172040 | tf_op jit(solution)/shard_map/ppermute | solution.py:344
  17.9 0.2 collective-permute-done
  18.1 1.6 collective-permute-done.1
  19.7 1.9 collective-permute-start.2
  21.7 5.1 %collective-permute-start.3 = (f32[7,6,4,128]{3,2,1,0:T(4,128)S(1)}, f32[7,6,4,128]{3,2,1,0:T(4,128)S(1)}, u32[]{:S(2)}, u32[]{:S(2)}) collective-permute-start(f32[7,6,4,128]{3,2,1,0:T(4,128)S(1)} %pad_maximum_fusion.1), channel_id=1, source_target_pairs={{1,0},{2,1},{3,2},{5,4},{6,5},{7,6},{9,8},{10,9},{11,10},{13,12},{... | collective-permute-start | bytes 258056 | tf_op jit(solution)/shard_map/ppermute | solution.py:344
  27.0 1.9 collective-permute-done.3.up
  28.9 32.3 %density.2.rho = f32[4,2,4,128]{3,2,1,0:T(4,128)S(1)} custom-call(f32[7,2,2,4,128]{4,3,2,1,0:T(4,128)S(1)} %copy.14.own, f32[7,2,2,4,128]{4,3,2,1,0:T(4,128)S(1)} %copy.15.left, f32[7,2,2,4,128]{4,3,2,1,0:T(4,128)S(1)} %copy.16.right, f32[7,6,4,128]{3,2,1,0:T(4,128)S(1)} %collective-permute-done.2.down, f32[7,6,4,128]{3,2,1,0:T(4,128)S(1)} %collective-permute-done.3.up), custom_call_target="tpu_custom_call" | custom-call | tf_op jit(solution)/shard_map/density/pallas_call | solution.py:303
  61.3 0.6 copy-done.11
  61.8 1.9 collective-permute-start.4
  63.8 5.2 %collective-permute-start.5 = (f32[4,4,128]{2,1,0:T(4,128)S(1)}, f32[4,4,128]{2,1,0:T(4,128)S(1)}, u32[]{:S(2)}, u32[]{:S(2)}) collective-permute-start(f32[4,4,128]{2,1,0:T(4,128)S(1)} %get-tuple-element.19), channel_id=1, source_target_pairs={{1,0},{2,1},{3,2},{5,4},{6,5},{7,6},{9,8},{10,9},{11,10},{13,12},{... | collective-permute-start | bytes 24584 | tf_op jit(solution)/shard_map/ppermute | solution.py:344
  69.0 1.3 collective-permute-done.5.rho_up
  70.3 0.6 copy-done.15
  70.9 41.8 %force.2.own = f32[7,2,2,4,128]{4,3,2,1,0:T(4,128)} custom-call(f32[7,2,2,4,128]{4,3,2,1,0:T(4,128)} %copy-done.1, f32[7,2,2,4,128]{4,3,2,1,0:T(4,128)} %copy-done.3, f32[7,2,2,4,128]{4,3,2,1,0:T(4,128)} %copy-done.5, f32[7,6,4,128]{3,2,1,0:T(4,128)} %copy-done.6, f32[7,6,4,128]{3,2,1,0:T(4,128)} %copy-done.8, f32[4,2,4,128]{3,2,1,0:T(4,128)} %copy-done.11, ...), custom_call_target="tpu_custom_call" | custom-call | tf_op jit(solution)/shard_map/force/pallas_call | solution.py:320
  112.8 0.9 copy.17
  113.7 1.9 collective-permute-start.6
  115.6 8.5 %collective-permute-start.7 = (f32[7,2,2,4,128]{4,3,1,0,2:T(4,128)S(1)}, f32[7,2,2,4,128]{4,3,1,0,2:T(4,128)S(1)}, u32[]{:S(2)}, u32[]{:S(2)}) collective-permute-start(f32[7,2,2,4,128]{4,3,1,0,2:T(4,128)S(1)} %copy.17), channel_id=1, source_target_pairs={{4,0},{8,4},{12,8},{16,12},{20,16},{24,20},{28,24},{32,28},{36,32}... | collective-permute-start | bytes 172040 | tf_op jit(solution)/shard_map/ppermute | solution.py:344
  124.1 0.2 collective-permute-done.6
  124.3 1.6 collective-permute-done.7
  125.9 4.9 %collective-permute-start.9 = (f32[7,6,4,128]{3,2,1,0:T(4,128)S(1)}, f32[7,6,4,128]{3,2,1,0:T(4,128)S(1)}, u32[]{:S(2)}, u32[]{:S(2)}) collective-permute-start(f32[7,6,4,128]{3,2,1,0:T(4,128)S(1)} %pad_maximum_fusion.3), channel_id=1, source_target_pairs={{1,0},{2,1},{3,2},{5,4},{6,5},{7,6},{9,8},{10,9},{11,10},{13,12},{... | collective-permute-start | bytes 258056 | tf_op jit(solution)/shard_map/ppermute | solution.py:344
  130.8 1.9 collective-permute-start.8
  132.9 5.3 %collective-permute-done.8.down = f32[7,6,4,128]{3,2,1,0:T(4,128)S(1)} collective-permute-done((f32[7,6,4,128]{3,2,1,0:T(4,128)S(1)}, f32[7,6,4,128]{3,2,1,0:T(4,128)S(1)}, u32[]{:S(2)}, u32[]{:S(2)}) %collective-permute-start.8) | collective-permute-done | bytes 86048 | tf_op jit(solution)/shard_map/ppermute | solution.py:339
  138.1 32.3 %density.3.rho = f32[4,2,4,128]{3,2,1,0:T(4,128)S(1)} custom-call(f32[7,2,2,4,128]{4,3,2,1,0:T(4,128)S(1)} %copy-done, f32[7,2,2,4,128]{4,3,2,1,0:T(4,128)S(1)} %copy.25.left, f32[7,2,2,4,128]{4,3,2,1,0:T(4,128)S(1)} %copy.26.right, f32[7,6,4,128]{3,2,1,0:T(4,128)S(1)} %collective-permute-done.8.down, f32[7,6,4,128]{3,2,1,0:T(4,128)S(1)} %collective-permute-done.9.up), custom_call_target="tpu_custom_call" | custom-call | tf_op jit(solution)/shard_map/density/pallas_call | solution.py:303
  170.5 1.9 collective-permute-start.10
  172.4 5.3 %collective-permute-start.11 = (f32[4,4,128]{2,1,0:T(4,128)S(1)}, f32[4,4,128]{2,1,0:T(4,128)S(1)}, u32[]{:S(2)}, u32[]{:S(2)}) collective-permute-start(f32[4,4,128]{2,1,0:T(4,128)S(1)} %get-tuple-element.17), channel_id=1, source_target_pairs={{1,0},{2,1},{3,2},{5,4},{6,5},{7,6},{9,8},{10,9},{11,10},{13,12},{... | collective-permute-start | bytes 24584 | tf_op jit(solution)/shard_map/ppermute | solution.py:344
  177.8 0.6 slice.94
  178.4 0.5 collective-permute-done.11.rho_up
  179.0 0.6 copy-done.14
  179.6 41.8 %force.3 = f32[7,2,2,4,128]{4,3,2,1,0:T(4,128)} custom-call(f32[7,2,2,4,128]{4,3,2,1,0:T(4,128)} %force.2.own, f32[7,2,2,4,128]{4,3,2,1,0:T(4,128)} %copy-done.2, f32[7,2,2,4,128]{4,3,2,1,0:T(4,128)} %copy-done.4, f32[7,6,4,128]{3,2,1,0:T(4,128)} %copy-done.9, f32[7,6,4,128]{3,2,1,0:T(4,128)} %copy-done.7, f32[4,2,4,128]{3,2,1,0:T(4,128)} %copy-done.10, ...), custom_call_target="tpu_custom_call" | custom-call | tf_op jit(solution)/shard_map/force/pallas_call | solution.py:320
  221.4 1.4 fusion.1
  (51 shorter events, 0.5 us)
Async XLA Ops:
  2.2 15.9 %collective-permute-start = (f32[7,2,2,4,128]{4,3,1,0,2:T(4,128)S(1)}, f32[7,2,2,4,128]{4,3,1,0,2:T(4,128)S(1)}, u32[]{:S(2)}, u32[]{:S(2)}) collective-permute-start(f32[7,2,2,4,128]{4,3,1,0,2:T(4,128)S(1)} %pad_maximum_fusion.4), channel_id=1, source_target_pairs={{0,4},{4,8},{8,12},{12,16},{16,20},{20,24},{24,28},{28,32},{32,36}... | collective-permute-start | bytes 172040 | tf_op jit(solution)/shard_map/ppermute | solution.py:339
  5.6 14.1 %collective-permute-start.1 = (f32[7,2,2,4,128]{4,3,1,0,2:T(4,128)S(1)}, f32[7,2,2,4,128]{4,3,1,0,2:T(4,128)S(1)}, u32[]{:S(2)}, u32[]{:S(2)}) collective-permute-start(f32[7,2,2,4,128]{4,3,1,0,2:T(4,128)S(1)} %pad_maximum_fusion.4), channel_id=1, source_target_pairs={{4,0},{8,4},{12,8},{16,12},{20,16},{24,20},{28,24},{32,28},{36,32}... | collective-permute-start | bytes 172040 | tf_op jit(solution)/shard_map/ppermute | solution.py:344
  19.7 7.3 %collective-permute-start.2 = (f32[7,6,4,128]{3,2,1,0:T(4,128)S(1)}, f32[7,6,4,128]{3,2,1,0:T(4,128)S(1)}, u32[]{:S(2)}, u32[]{:S(2)}) collective-permute-start(f32[7,6,4,128]{3,2,1,0:T(4,128)S(1)} %pad_maximum_fusion), channel_id=1, source_target_pairs={{0,1},{1,2},{2,3},{4,5},{5,6},{6,7},{8,9},{9,10},{10,11},{12,13},{... | collective-permute-start | bytes 258056 | tf_op jit(solution)/shard_map/ppermute | solution.py:339
  21.7 7.2 %collective-permute-start.3 = (f32[7,6,4,128]{3,2,1,0:T(4,128)S(1)}, f32[7,6,4,128]{3,2,1,0:T(4,128)S(1)}, u32[]{:S(2)}, u32[]{:S(2)}) collective-permute-start(f32[7,6,4,128]{3,2,1,0:T(4,128)S(1)} %pad_maximum_fusion.1), channel_id=1, source_target_pairs={{1,0},{2,1},{3,2},{5,4},{6,5},{7,6},{9,8},{10,9},{11,10},{13,12},{... | collective-permute-start | bytes 258056 | tf_op jit(solution)/shard_map/ppermute | solution.py:344
  26.8 2.1 copy-start.1
  26.9 2.0 copy-start.3
  26.9 34.3 %copy-start.5 = (f32[7,2,2,4,128]{4,3,2,1,0:T(4,128)}, f32[7,2,2,4,128]{4,3,2,1,0:T(4,128)S(1)}, u32[]{:S(2)}) copy-start(f32[7,2,2,4,128]{4,3,2,1,0:T(4,128)S(1)} %copy.16.right) | copy-start | bytes 172036
  27.0 34.2 %copy-start.6 = (f32[7,6,4,128]{3,2,1,0:T(4,128)}, f32[7,6,4,128]{3,2,1,0:T(4,128)S(1)}, u32[]{:S(2)}) copy-start(f32[7,6,4,128]{3,2,1,0:T(4,128)S(1)} %collective-permute-done.2.down) | copy-start | bytes 258052
  28.9 32.3 %copy-start.8 = (f32[7,6,4,128]{3,2,1,0:T(4,128)}, f32[7,6,4,128]{3,2,1,0:T(4,128)S(1)}, u32[]{:S(2)}) copy-start(f32[7,6,4,128]{3,2,1,0:T(4,128)S(1)} %collective-permute-done.3.up) | copy-start | bytes 258052
  61.2 0.6 copy-start.11
  61.8 7.2 %collective-permute-start.4 = (f32[4,4,128]{2,1,0:T(4,128)S(1)}, f32[4,4,128]{2,1,0:T(4,128)S(1)}, u32[]{:S(2)}, u32[]{:S(2)}) collective-permute-start(f32[4,4,128]{2,1,0:T(4,128)S(1)} %get-tuple-element.20), channel_id=1, source_target_pairs={{0,1},{1,2},{2,3},{4,5},{5,6},{6,7},{8,9},{9,10},{10,11},{12,13},{... | collective-permute-start | bytes 24584 | tf_op jit(solution)/shard_map/ppermute | solution.py:339
  63.8 6.6 %collective-permute-start.5 = (f32[4,4,128]{2,1,0:T(4,128)S(1)}, f32[4,4,128]{2,1,0:T(4,128)S(1)}, u32[]{:S(2)}, u32[]{:S(2)}) collective-permute-start(f32[4,4,128]{2,1,0:T(4,128)S(1)} %get-tuple-element.19), channel_id=1, source_target_pairs={{1,0},{2,1},{3,2},{5,4},{6,5},{7,6},{9,8},{10,9},{11,10},{13,12},{... | collective-permute-start | bytes 24584 | tf_op jit(solution)/shard_map/ppermute | solution.py:344
  69.0 1.3 copy-start.13
  70.3 0.6 copy-start.15
  112.8 11.3 %copy-start = (f32[7,2,2,4,128]{4,3,2,1,0:T(4,128)S(1)}, f32[7,2,2,4,128]{4,3,2,1,0:T(4,128)}, u32[]{:S(2)}) copy-start(f32[7,2,2,4,128]{4,3,2,1,0:T(4,128)} %force.2.own) | copy-start | bytes 172036
  113.7 10.6 %collective-permute-start.6 = (f32[7,2,2,4,128]{4,3,1,0,2:T(4,128)S(1)}, f32[7,2,2,4,128]{4,3,1,0,2:T(4,128)S(1)}, u32[]{:S(2)}, u32[]{:S(2)}) collective-permute-start(f32[7,2,2,4,128]{4,3,1,0,2:T(4,128)S(1)} %copy.17), channel_id=1, source_target_pairs={{0,4},{4,8},{8,12},{12,16},{16,20},{20,24},{24,28},{28,32},{32,36}... | collective-permute-start | bytes 172040 | tf_op jit(solution)/shard_map/ppermute | solution.py:339
  115.6 10.3 %collective-permute-start.7 = (f32[7,2,2,4,128]{4,3,1,0,2:T(4,128)S(1)}, f32[7,2,2,4,128]{4,3,1,0,2:T(4,128)S(1)}, u32[]{:S(2)}, u32[]{:S(2)}) collective-permute-start(f32[7,2,2,4,128]{4,3,1,0,2:T(4,128)S(1)} %copy.17), channel_id=1, source_target_pairs={{4,0},{8,4},{12,8},{16,12},{20,16},{24,20},{28,24},{32,28},{36,32}... | collective-permute-start | bytes 172040 | tf_op jit(solution)/shard_map/ppermute | solution.py:344
  125.9 7.0 %collective-permute-start.9 = (f32[7,6,4,128]{3,2,1,0:T(4,128)S(1)}, f32[7,6,4,128]{3,2,1,0:T(4,128)S(1)}, u32[]{:S(2)}, u32[]{:S(2)}) collective-permute-start(f32[7,6,4,128]{3,2,1,0:T(4,128)S(1)} %pad_maximum_fusion.3), channel_id=1, source_target_pairs={{1,0},{2,1},{3,2},{5,4},{6,5},{7,6},{9,8},{10,9},{11,10},{13,12},{... | collective-permute-start | bytes 258056 | tf_op jit(solution)/shard_map/ppermute | solution.py:344
  130.8 7.3 %collective-permute-start.8 = (f32[7,6,4,128]{3,2,1,0:T(4,128)S(1)}, f32[7,6,4,128]{3,2,1,0:T(4,128)S(1)}, u32[]{:S(2)}, u32[]{:S(2)}) collective-permute-start(f32[7,6,4,128]{3,2,1,0:T(4,128)S(1)} %pad_maximum_fusion.2), channel_id=1, source_target_pairs={{0,1},{1,2},{2,3},{4,5},{5,6},{6,7},{8,9},{9,10},{10,11},{12,13},{... | collective-permute-start | bytes 258056 | tf_op jit(solution)/shard_map/ppermute | solution.py:339
  132.8 5.4 %copy-start.2 = (f32[7,2,2,4,128]{4,3,2,1,0:T(4,128)}, f32[7,2,2,4,128]{4,3,2,1,0:T(4,128)S(1)}, u32[]{:S(2)}) copy-start(f32[7,2,2,4,128]{4,3,2,1,0:T(4,128)S(1)} %copy.25.left) | copy-start | bytes 172036
  132.8 37.6 %copy-start.4 = (f32[7,2,2,4,128]{4,3,2,1,0:T(4,128)}, f32[7,2,2,4,128]{4,3,2,1,0:T(4,128)S(1)}, u32[]{:S(2)}) copy-start(f32[7,2,2,4,128]{4,3,2,1,0:T(4,128)S(1)} %copy.26.right) | copy-start | bytes 172036
  132.9 37.6 %copy-start.7 = (f32[7,6,4,128]{3,2,1,0:T(4,128)}, f32[7,6,4,128]{3,2,1,0:T(4,128)S(1)}, u32[]{:S(2)}) copy-start(f32[7,6,4,128]{3,2,1,0:T(4,128)S(1)} %collective-permute-done.9.up) | copy-start | bytes 258052
  138.1 32.3 %copy-start.9 = (f32[7,6,4,128]{3,2,1,0:T(4,128)}, f32[7,6,4,128]{3,2,1,0:T(4,128)S(1)}, u32[]{:S(2)}) copy-start(f32[7,6,4,128]{3,2,1,0:T(4,128)S(1)} %collective-permute-done.8.down) | copy-start | bytes 258052
  170.5 7.3 %copy-start.10 = (f32[4,2,4,128]{3,2,1,0:T(4,128)}, f32[4,2,4,128]{3,2,1,0:T(4,128)S(1)}, u32[]{:S(2)}) copy-start(f32[4,2,4,128]{3,2,1,0:T(4,128)S(1)} %density.3.rho) | copy-start | bytes 49156
  170.5 7.9 %collective-permute-start.10 = (f32[4,4,128]{2,1,0:T(4,128)S(1)}, f32[4,4,128]{2,1,0:T(4,128)S(1)}, u32[]{:S(2)}, u32[]{:S(2)}) collective-permute-start(f32[4,4,128]{2,1,0:T(4,128)S(1)} %get-tuple-element.18), channel_id=1, source_target_pairs={{0,1},{1,2},{2,3},{4,5},{5,6},{6,7},{8,9},{9,10},{10,11},{12,13},{... | collective-permute-start | bytes 24584 | tf_op jit(solution)/shard_map/ppermute | solution.py:339
  172.4 6.5 %collective-permute-start.11 = (f32[4,4,128]{2,1,0:T(4,128)S(1)}, f32[4,4,128]{2,1,0:T(4,128)S(1)}, u32[]{:S(2)}, u32[]{:S(2)}) collective-permute-start(f32[4,4,128]{2,1,0:T(4,128)S(1)} %get-tuple-element.17), channel_id=1, source_target_pairs={{1,0},{2,1},{3,2},{5,4},{6,5},{7,6},{9,8},{10,9},{11,10},{13,12},{... | collective-permute-start | bytes 24584 | tf_op jit(solution)/shard_map/ppermute | solution.py:344
  178.4 0.6 copy-start.12
  179.0 0.6 copy-start.14

commit v2 on v1

v2 whole, which is shorter than its diff:
```python
import functools
import math

import jax
import jax.numpy as jnp
from jax import lax
from jax.experimental import pallas as pl
from jax.experimental.pallas import tpu as pltpu
from jax.sharding import PartitionSpec as P

STEPS = 2
SLOTS = 128
MASS = 8.0 / SLOTS
KERNEL_NORM = 21.0 / (16.0 * math.pi)
TAIT = 10.0 * 10.0 / 7.0
TIME_STEP = 0.02
GRAVITY = 1.0
FAR = 1000.0
TINY = 1e-30

PARTS_J = (0, 0, 1, 1, 0, 2)
PARTS_I = (0, 1, 0, 1, 2, 0)
ROW_X = 0
ROW_NJ = 18
ROW_ONE = 21
ROW_V = 24
ROW_WJ = 42
ROW_RHO = 45
ROW_P = 48
SHORT = 32
LONG = 64
DEPTH = 128
SUM_ROWS = ((ROW_X, ROW_X + 2, ROW_X + 5), (ROW_X + 6, ROW_X + 8, ROW_X + 11), (ROW_X + 12, ROW_X + 14, ROW_X + 17))


def split3(value):
    high = value.astype(jnp.bfloat16).astype(jnp.float32)
    rest = value - high
    middle = rest.astype(jnp.bfloat16).astype(jnp.float32)
    return (high, middle, rest - middle)


def dot(lhs, rhs):
    return jnp.dot(lhs, rhs, preferred_element_type=jnp.float32)


def fold(tile):
    return jnp.sum(tile.reshape(tile.shape[0] // 8, 8, tile.shape[1]), axis=0)


def parities():
    return lax.axis_index("slab") % 2 == 0, lax.axis_index("col") % 2 == 0


def column_of(refs, comp, ix, iy):
    own, slab_a, slab_b, col_a, col_b = refs
    slab_even, col_even = parities()
    if iy in (0, 3):
        near, other = (col_b, col_a) if iy == 0 else (col_a, col_b)
        rows = lambda at: jnp.where(col_even, near[comp, at], other[comp, at])
        if 2 <= ix < 4:
            return rows(ix)
        at_a, at_b = ix % 2, 4 + ix % 2
        first, second = (at_b, at_a) if ix < 2 else (at_a, at_b)
        return jnp.where(slab_even, rows(first), rows(second))
    if 2 <= ix < 4:
        return own[comp, ix - 2, iy - 1]
    first, second = (slab_b, slab_a) if ix < 2 else (slab_a, slab_b)
    return jnp.where(slab_even, first[comp, ix % 2, iy - 1], second[comp, ix % 2, iy - 1])


def centred(refs, ix, iy):
    places = []
    for axis in range(3):
        half = 0.5 * column_of(refs, axis, ix, iy)
        if axis == 2:
            shift = lax.broadcasted_iota(jnp.int32, half.shape, 0).astype(jnp.float32) - 0.5 * half.shape[0]
        else:
            shift = (ix - 3.0, iy - 2.0)[axis]
        places.append(half + shift)
    return places


def source_rows(refs, ix, iy, with_velocity):
    live = column_of(refs, 6, ix, iy) > 0.5
    places = [jnp.where(live, place, FAR) for place in centred(refs, ix, iy)]
    rows = {}
    for axis in range(3):
        parts = split3(places[axis])
        for at, part in enumerate(PARTS_J):
            rows[ROW_X + 6 * axis + at] = parts[part]
    norm = places[0] * places[0] + places[1] * places[1] + places[2] * places[2]
    for at, part in enumerate(split3(norm)):
        rows[ROW_NJ + at] = part
        rows[ROW_ONE + at] = jnp.ones_like(part)
    if with_velocity:
        speeds = [column_of(refs, 3 + axis, ix, iy) for axis in range(3)]
        along = 0.0
        for axis in range(3):
            parts = split3(speeds[axis])
            for at, part in enumerate(PARTS_J):
                rows[ROW_V + 6 * axis + at] = parts[part]
            along = along + speeds[axis] * places[axis]
        for at, part in enumerate(split3(along)):
            rows[ROW_WJ + at] = part
    return rows


def put_rows(table, column, rows, depth):
    blank = jnp.zeros((table.shape[1], SLOTS), jnp.float32)
    for row in range(depth):
        table[column, :, row, :] = rows.get(row, blank)


def turned_cell(table, column, z):
    rows = table[column, z]
    flat = jnp.transpose(rows)
    return jnp.concatenate([flat, jnp.zeros((SLOTS, DEPTH - rows.shape[0]), jnp.float32)], axis=1).astype(jnp.bfloat16)


def deep(rows):
    return jnp.concatenate([rows, jnp.zeros((DEPTH - rows.shape[0], SLOTS), jnp.float32)], axis=0).astype(jnp.bfloat16)


def density_kernel(own, slab_a, slab_b, col_a, col_b, rho_ref, send_a, send_b, table, turned, weights):
    refs = (own, slab_a, slab_b, col_a, col_b)
    cells_z = own.shape[3]
    for ix in range(6):
        for iy in range(4):
            put_rows(table, ix * 4 + iy, source_rows(refs, ix, iy, False), SHORT)

    def turn(column, carry):
        for z in range(cells_z):
            turned[column, z] = turned_cell(table, column, z)
        return carry

    lax.fori_loop(0, 24, turn, 0)
    for tx in range(4):
        for ty in range(2):
            places = centred(refs, tx + 1, ty + 1)
            rows = {}
            for axis in range(3):
                parts = split3(-2.0 * places[axis])
                for at, part in enumerate(PARTS_I):
                    rows[ROW_X + 6 * axis + at] = parts[part]
            norm = places[0] * places[0] + places[1] * places[1] + places[2] * places[2]
            for at, part in enumerate(split3(norm)):
                rows[ROW_NJ + at] = jnp.ones_like(part)
                rows[ROW_ONE + at] = part
            put_rows(weights, tx * 2 + ty, rows, SHORT)

    def target(step, carry):
        tx, ty = step // 2, step % 2
        rhs = [
            jnp.concatenate([deep(weights[step, 2 * pair]), deep(weights[step, 2 * pair + 1])], axis=1)
            for pair in range(cells_z // 2)
        ]

        def source(dx, sums):
            sums = list(sums)
            for dy in range(3):
                column = (tx + dx) * 4 + ty + dy
                for pair in range(cells_z // 2):
                    for z in range(max(0, 2 * pair - 1), min(cells_z, 2 * pair + 3)):
                        gap = dot(turned[column, z], rhs[pair])
                        for half in range(2):
                            zt = 2 * pair + half
                            if abs(zt - z) > 1:
                                continue
                            near = jnp.maximum(gap[:, half * SLOTS : (half + 1) * SLOTS], TINY)
                            inside = jnp.maximum(1.0 - near * lax.rsqrt(near), 0.0)
                            square = inside * inside
                            fourth = square * square
                            sums[2 * zt] = sums[2 * zt] + fold(fourth)
                            sums[2 * zt + 1] = sums[2 * zt + 1] + fold(fourth * inside)
            return tuple(sums)

        zero = jnp.zeros((8, SLOTS), jnp.float32)
        sums = lax.fori_loop(0, 3, source, (zero,) * (2 * cells_z))
        for zt in range(cells_z):
            total = 5.0 * sums[2 * zt] - 4.0 * sums[2 * zt + 1]
            rho_ref[tx, ty, pl.ds(zt, 1), :] = (MASS * KERNEL_NORM) * jnp.sum(total, axis=0, keepdims=True)
        return carry

    lax.fori_loop(0, 8, target, 0)
    for ix in range(2):
        for iy in range(2):
            rho_ref[ix + 1, iy] = rho_ref[ix + 1, iy] + (1.0 - own[6, ix, iy]) * (MASS * KERNEL_NORM)
    col_even = parities()[1]
    for ix in range(4):
        low, high = rho_ref[ix, 0], rho_ref[ix, 1]
        send_a[ix] = jnp.where(col_even, high, low)
        send_b[ix] = jnp.where(col_even, low, high)


def pressure_ratio(density):
    cubed = density * density * density
    return TAIT * (cubed * cubed * density - 1.0) / (density * density)


def force_kernel(
    last, own, slab_a, slab_b, col_a, col_b, rho, rho_a, rho_b, place_ref, speed_ref, table, turned, weights, spread, rows_i
):
    refs = (own, slab_a, slab_b, col_a, col_b)
    cells_z = own.shape[3]
    col_even = parities()[1]
    for ix in range(4):
        for iy in range(4):
            rows = source_rows(refs, ix + 1, iy, True)
            if iy == 0:
                density = jnp.where(col_even, rho_b[ix], rho_a[ix])
            elif iy == 3:
                density = jnp.where(col_even, rho_a[ix], rho_b[ix])
            else:
                density = rho[ix, iy - 1]
            density = jnp.maximum(density, MASS * KERNEL_NORM)
            for at, part in enumerate(split3(density)):
                rows[ROW_RHO + at] = part
            for at, part in enumerate(split3(pressure_ratio(density))):
                rows[ROW_P + at] = part
            put_rows(table, ix * 4 + iy, rows, LONG)

    at_row = lax.broadcasted_iota(jnp.int32, (DEPTH, SLOTS), 0)
    picks = []
    for rows in SUM_ROWS + (tuple(range(ROW_RHO, ROW_RHO + 3)), tuple(range(ROW_P, ROW_P + 3))):
        chosen = (at_row == rows[0]) | (at_row == rows[1]) | (at_row == rows[2])
        picks.append(jnp.where(chosen, 1.0, 0.0).astype(jnp.bfloat16))

    def turn(column, carry):
        for z in range(cells_z):
            flat = turned_cell(table, column, z)
            turned[column, z] = flat
            for at, pick in enumerate(picks):
                spread[column, z, at] = dot(flat, pick)
        return carry

    lax.fori_loop(0, 16, turn, 0)

    for tx in range(2):
        for ty in range(2):
            places = centred(refs, tx + 2, ty + 1)
            speeds = [column_of(refs, 3 + axis, tx + 2, ty + 1) for axis in range(3)]
            gap_rows, near_rows = {}, {}
            norm, along = 0.0, 0.0
            for axis in range(3):
                gap_parts = split3(-2.0 * places[axis])
                place_parts = split3(2.0 * places[axis])
                speed_parts = split3(2.0 * speeds[axis])
                for at, part in enumerate(PARTS_I):
                    gap_rows[ROW_X + 6 * axis + at] = gap_parts[part]
                    near_rows[ROW_X + 6 * axis + at] = speed_parts[part]
                    near_rows[ROW_V + 6 * axis + at] = place_parts[part]
                norm = norm + places[axis] * places[axis]
                along = along + places[axis] * speeds[axis]
            for at, (part, other) in enumerate(zip(split3(norm), split3(-2.0 * along))):
                gap_rows[ROW_NJ + at] = jnp.ones_like(part)
                gap_rows[ROW_ONE + at] = part
                near_rows[ROW_WJ + at] = jnp.full_like(part, -2.0)
                near_rows[ROW_ONE + at] = other
            put_rows(weights.at[0], tx * 2 + ty, gap_rows, LONG)
            put_rows(weights.at[1], tx * 2 + ty, near_rows, LONG)
            density = jnp.maximum(rho[tx + 1, ty], MASS * KERNEL_NORM)
            rows_i[tx * 2 + ty, 0] = density
            rows_i[tx * 2 + ty, 1] = pressure_ratio(density)
            for axis in range(3):
                rows_i[tx * 2 + ty, 2 + axis] = places[axis]

    def target(step, carry):
        tx, ty = step // 2, step % 2
        rhs = [jnp.concatenate([deep(weights[0, step, z]), deep(weights[1, step, z])], axis=1) for z in range(cells_z)]
        rho_i = [rows_i[step, 0, pl.ds(z, 1), :] for z in range(cells_z)]
        ratio_i = [rows_i[step, 1, pl.ds(z, 1), :] for z in range(cells_z)]

        def source(dx, sums):
            sums = list(sums)
            for dy in range(3):
                column = (tx + dx) * 4 + ty + dy
                for zt in range(cells_z):
                    for z in range(max(0, zt - 1), min(cells_z, zt + 2)):
                        both = dot(turned[column, z], rhs[zt])
                        near = jnp.maximum(both[:, :SLOTS], TINY)
                        inside = jnp.maximum(1.0 - near * lax.rsqrt(near), 0.0)
                        closing = jnp.maximum(both[:, SLOTS:], 0.0)
                        below = (near + 0.0025) * (spread[column, z, 3] + rho_i[zt])
                        strength = (spread[column, z, 4] + ratio_i[zt]) + closing / below
                        strength = strength * (inside * inside * inside)
                        for axis in range(3):
                            sums[4 * zt + axis] = sums[4 * zt + axis] + fold(strength * spread[column, z, axis])
                        sums[4 * zt + 3] = sums[4 * zt + 3] + fold(strength)
            return tuple(sums)

        zero = jnp.zeros((8, SLOTS), jnp.float32)
        sums = lax.fori_loop(0, 3, source, (zero,) * (4 * cells_z))
        for zt in range(cells_z):
            row = pl.ds(zt, 1)
            *parts, whole = [jnp.sum(total, axis=0, keepdims=True) for total in sums[4 * zt : 4 * zt + 4]]
            live = own[6, tx, ty, row, :] > 0.5
            for axis in range(3):
                pull = (10.0 * KERNEL_NORM * MASS) * (rows_i[step, 2 + axis, row, :] * whole - parts[axis])
                if axis == 2:
                    pull = pull - GRAVITY
                old_place = own[axis, tx, ty, row, :]
                old_speed = own[3 + axis, tx, ty, row, :]
                speed = old_speed + TIME_STEP * pull
                place_ref[axis, tx, ty, row, :] = jnp.where(live, old_place + TIME_STEP * speed, old_place)
                speed_at = axis if last else 3 + axis
                speed_ref[speed_at, tx, ty, row, :] = jnp.where(live, speed, old_speed)
            if not last:
                place_ref[6, tx, ty, row, :] = own[6, tx, ty, row, :]
        return carry

    lax.fori_loop(0, 4, target, 0)


def middle_force_kernel(own, a, b, c, d, rho, rho_a, rho_b, out_ref, *scratch):
    force_kernel(False, own, a, b, c, d, rho, rho_a, rho_b, out_ref, out_ref, *scratch)


VMEM_SPEC = pl.BlockSpec(memory_space=pltpu.VMEM)


def shaped(*shape):
    return jax.ShapeDtypeStruct(shape, jnp.float32)


def densities(state, slab_a, slab_b, col_a, col_b):
    cells_z = state.shape[3]
    return pl.pallas_call(
        density_kernel,
        name="density",
        out_shape=(shaped(4, 2, cells_z, SLOTS), shaped(4, cells_z, SLOTS), shaped(4, cells_z, SLOTS)),
        in_specs=[VMEM_SPEC] * 5,
        out_specs=(VMEM_SPEC,) * 3,
        scratch_shapes=[
            pltpu.VMEM((24, cells_z, SHORT, SLOTS), jnp.float32),
            pltpu.VMEM((24, cells_z, SLOTS, DEPTH), jnp.bfloat16),
            pltpu.VMEM((8, cells_z, SHORT, SLOTS), jnp.float32),
        ],
        compiler_params=pltpu.CompilerParams(vmem_limit_bytes=32 << 20),
    )(state, slab_a, slab_b, col_a, col_b)


def moved(last, state, slab_a, slab_b, col_a, col_b, rho, rho_a, rho_b):
    cells_z = state.shape[3]
    block = state.shape[1:]
    return pl.pallas_call(
        functools.partial(force_kernel, True) if last else middle_force_kernel,
        name="force",
        out_shape=(shaped(3, *block), shaped(3, *block)) if last else shaped(7, *block),
        in_specs=[VMEM_SPEC] * 8,
        out_specs=(VMEM_SPEC, VMEM_SPEC) if last else VMEM_SPEC,
        scratch_shapes=[
            pltpu.VMEM((16, cells_z, LONG, SLOTS), jnp.float32),
            pltpu.VMEM((16, cells_z, SLOTS, DEPTH), jnp.bfloat16),
            pltpu.VMEM((2, 4, cells_z, LONG, SLOTS), jnp.float32),
            pltpu.VMEM((16, cells_z, 5, SLOTS, SLOTS), jnp.float32),
            pltpu.VMEM((4, 5, cells_z, SLOTS), jnp.float32),
        ],
        compiler_params=pltpu.CompilerParams(vmem_limit_bytes=40 << 20),
    )(state, slab_a, slab_b, col_a, col_b, rho, rho_a, rho_b)


def swap_even(value, axis):
    return lax.ppermute(value, axis, [(i, i ^ 1) for i in range(lax.axis_size(axis))])


def swap_odd(value, axis):
    count = lax.axis_size(axis)
    return lax.ppermute(value, axis, [(i, i - 1 if i % 2 == 0 else i + 1) for i in range(1, count - 1)])


def per_device(offsets, velocity, occupancy):
    slot_rank = jnp.arange(SLOTS, dtype=jnp.int32)
    live = (slot_rank < occupancy[..., None]).astype(jnp.float32)
    state = jnp.concatenate([offsets, velocity, live[None]], axis=0)
    col_odd = lax.axis_index("col") % 2
    for section in range(STEPS):
        slab_b, slab_a = swap_odd(state, "slab"), swap_even(state, "slab")
        edges = [
            jnp.concatenate([lax.dynamic_index_in_dim(part, y, 2, keepdims=False) for part in (slab_a, state, slab_b)], axis=1)
            for y in (col_odd, 1 - col_odd)
        ]
        col_b, col_a = swap_odd(edges[0], "col"), swap_even(edges[1], "col")
        rho, rho_a, rho_b = densities(state, slab_a, slab_b, col_a, col_b)
        rho_b, rho_a = swap_odd(rho_b, "col"), swap_even(rho_a, "col")
        state = moved(section == STEPS - 1, state, slab_a, slab_b, col_a, col_b, rho, rho_a, rho_b)
    return (state[0], state[1], rho[1:3])


def solution(mesh):
    placed = P(None, "slab", "col", None, None)
    return jax.shard_map(
        per_device,
        mesh=mesh,
        in_specs=(placed, placed, P("slab", "col", None)),
        out_specs=(placed, placed, P("slab", "col", None, None)),
        check_vma=False,
    )
```

time: 226 us -> 174 us (0.77); the launches traced: 223 us -> 174 us
  Pallas kernels: 148 us -> 106 us
  starting transfers between devices: 54.3 us -> 39.4 us
  waiting for transfers between devices: 12.7 us -> 25.2 us
  local copies, waits for them, and re-layouts: 5.55 us -> 0.69 us
    pallas_call x4, Pallas kernels: 148 us -> 106 us  [the longest x2 57.3 us: moved(): pl.pallas_call(functools.partial(force_kernel, True) if last else middle_...]
    ppermute x12, starting transfers between devices: 54.3 us -> 39.4 us  [the longest x6 27.9 us: swap_odd(): lax.ppermute(value, axis, [(i, i - 1 if i % 2 == 0 else i + 1) for i in r...]
    ppermute x12, waiting for transfers between devices: 12.7 us -> 25.2 us  [the longest x6 21.2 us: swap_odd(): lax.ppermute(value, axis, [(i, i - 1 if i % 2 == 0 else i + 1) for i in r...]
    unnamed x33 -> x0, local copies, waits for them, and re-layouts: 2.57 us -> none
  transfers between devices with their start and end apart: 12 -> 12, of which waited for: 10 -> 7; matrix products, arithmetic and copies ran while one was open for 0% -> 0% of each run, Pallas kernels for 0% -> 0%
where the time goes in v2:
time: 174 us
  Pallas kernels  106 us (61%)
  starting transfers between devices  39.4 us (23%)
  waiting for transfers between devices  25.2 us (14%)
    pallas_call x2, Pallas kernels, moved(): pl.pallas_call(functools.partial(force_kernel, True) if last else middle_...  57.3 us
    pallas_call x2, Pallas kernels, densities(): pl.pallas_call(density_kernel, name='density', out_shape=(shaped(4, 2, ce...  48.8 us
    ppermute x6, starting transfers between devices, swap_odd(): lax.ppermute(value, axis, [(i, i - 1 if i % 2 == 0 else i + 1) for i in r...  27.9 us
    ppermute x6, waiting for transfers between devices, swap_odd(): lax.ppermute(value, axis, [(i, i - 1 if i % 2 == 0 else i + 1) for i in r...  21.2 us
    ppermute x6, starting transfers between devices, swap_even(): lax.ppermute(value, axis, [(i, i ^ 1) for i in range(lax.axis_size(axis))])  11.5 us
    ppermute x6, waiting for transfers between devices, swap_even(): lax.ppermute(value, axis, [(i, i ^ 1) for i in range(lax.axis_size(axis))])  3.93 us
  transfers between devices with their start and end apart: 12, of which 7 were waited for; matrix products, arithmetic and copies ran while one was open for 0% of the time, Pallas kernels for 0%

profile of v2, /device:TPU:24, one launch (start us, length us, event | category | flops | bytes accessed | tf_op | source)
XLA Modules:
  0.0 173.9 jit_solution(4533549522269824072)
XLA Ops:
  0.6 0.8 fusion
  1.4 0.8 pad_maximum_fusion.4.own
  2.2 13.8 %collective-permute-start.1 = (f32[7,2,2,4,128]{4,3,2,1,0:T(4,128)S(1)}, f32[7,2,2,4,128]{4,3,2,1,0:T(4,128)S(1)}, u32[]{:S(2)}, u32[]{:S(2)}) collective-permute-start(f32[7,2,2,4,128]{4,3,2,1,0:T(4,128)S(1)} %pad_maximum_fusion.4.own), channel_id=1, source_target_pairs={{4,8},{8,4},{12,16},{16,12},{20,24},{24,20},{28,32},{32,28},{36,40... | collective-permute-start | bytes 172040 | tf_op jit(solution)/shard_map/ppermute | solution.py:369
  15.9 1.9 %collective-permute-start = (f32[7,2,2,4,128]{4,3,2,1,0:T(4,128)S(1)}, f32[7,2,2,4,128]{4,3,2,1,0:T(4,128)S(1)}, u32[]{:S(2)}, u32[]{:S(2)}) collective-permute-start(f32[7,2,2,4,128]{4,3,2,1,0:T(4,128)S(1)} %pad_maximum_fusion.4.own), channel_id=1, source_target_pairs={{0,4},{4,0},{8,12},{12,8},{16,20},{20,16},{24,28},{28,24},{32,36},... | collective-permute-start | bytes 172040 | tf_op jit(solution)/shard_map/ppermute | solution.py:364
  17.9 0.2 collective-permute-done.1.slab_b.b
  18.1 3.9 %collective-permute-done.slab_a.a = f32[7,2,2,4,128]{4,3,2,1,0:T(4,128)S(1)} collective-permute-done((f32[7,2,2,4,128]{4,3,2,1,0:T(4,128)S(1)}, f32[7,2,2,4,128]{4,3,2,1,0:T(4,128)S(1)}, u32[]{:S(2)}, u32[]{:S(2)}) %collective-permute-start) | collective-permute-done | bytes 57376 | tf_op jit(solution)/shard_map/ppermute | solution.py:364
  22.1 1.9 %collective-permute-start.2 = (f32[7,6,4,128]{3,2,1,0:T(4,128)S(1)}, f32[7,6,4,128]{3,2,1,0:T(4,128)S(1)}, u32[]{:S(2)}, u32[]{:S(2)}) collective-permute-start(f32[7,6,4,128]{3,2,1,0:T(4,128)S(1)} %pad_maximum_fusion), channel_id=1, source_target_pairs={{0,1},{1,0},{2,3},{3,2},{4,5},{5,4},{6,7},{7,6},{8,9},{9,8},{10,11... | collective-permute-start | bytes 258056 | tf_op jit(solution)/shard_map/ppermute | solution.py:364
  24.0 3.0 %collective-permute-start.3 = (f32[7,6,4,128]{3,2,1,0:T(4,128)S(1)}, f32[7,6,4,128]{3,2,1,0:T(4,128)S(1)}, u32[]{:S(2)}, u32[]{:S(2)}) collective-permute-start(f32[7,6,4,128]{3,2,1,0:T(4,128)S(1)} %pad_maximum_fusion.1), channel_id=1, source_target_pairs={{1,2},{2,1},{5,6},{6,5},{9,10},{10,9},{13,14},{14,13},{17,18},{18,... | collective-permute-start | bytes 258056 | tf_op jit(solution)/shard_map/ppermute | solution.py:369
  27.0 0.0 collective-permute-done.2.col_a.c
  27.0 4.3 %collective-permute-done.3.col_b.d = f32[7,6,4,128]{3,2,1,0:T(4,128)S(1)} collective-permute-done((f32[7,6,4,128]{3,2,1,0:T(4,128)S(1)}, f32[7,6,4,128]{3,2,1,0:T(4,128)S(1)}, u32[]{:S(2)}, u32[]{:S(2)}) %collective-permute-start.3) | collective-permute-done | bytes 86048 | tf_op jit(solution)/shard_map/ppermute | solution.py:369
  31.3 24.4 %density.2 = (f32[4,2,4,128]{3,2,1,0:T(4,128)S(1)}, f32[4,4,128]{2,1,0:T(4,128)S(1)}, f32[4,4,128]{2,1,0:T(4,128)S(1)}) custom-call(f32[7,2,2,4,128]{4,3,2,1,0:T(4,128)S(1)} %pad_maximum_fusion.4.own, f32[7,2,2,4,128]{4,3,2,1,0:T(4,128)S(1)} %collective-permute-done.slab_a.a, f32[7,2,2,4,128]{4,3,2,1,0:T(4,128)S(1)} %collective-permute-done.1.slab_b.b, ...), custom_call_target="tpu_custom_call" | custom-call | tf_op jit(solution)/shard_map/density/pallas_call | solution.py:328
  55.7 1.9 %collective-permute-start.4 = (f32[4,4,128]{2,1,0:T(4,128)S(1)}, f32[4,4,128]{2,1,0:T(4,128)S(1)}, u32[]{:S(2)}, u32[]{:S(2)}) collective-permute-start(f32[4,4,128]{2,1,0:T(4,128)S(1)} %get-tuple-element.12), channel_id=1, source_target_pairs={{0,1},{1,0},{2,3},{3,2},{4,5},{5,4},{6,7},{7,6},{8,9},{9,8},{10,11... | collective-permute-start | bytes 24584 | tf_op jit(solution)/shard_map/ppermute | solution.py:364
  57.7 3.0 %collective-permute-start.5 = (f32[4,4,128]{2,1,0:T(4,128)S(1)}, f32[4,4,128]{2,1,0:T(4,128)S(1)}, u32[]{:S(2)}, u32[]{:S(2)}) collective-permute-start(f32[4,4,128]{2,1,0:T(4,128)S(1)} %get-tuple-element.13), channel_id=1, source_target_pairs={{1,2},{2,1},{5,6},{6,5},{9,10},{10,9},{13,14},{14,13},{17,18},{18,... | collective-permute-start | bytes 24584 | tf_op jit(solution)/shard_map/ppermute | solution.py:369
  60.6 0.0 collective-permute-done.4.rho_a
  60.6 3.5 %collective-permute-done.5.rho_b = f32[4,4,128]{2,1,0:T(4,128)S(1)} collective-permute-done((f32[4,4,128]{2,1,0:T(4,128)S(1)}, f32[4,4,128]{2,1,0:T(4,128)S(1)}, u32[]{:S(2)}, u32[]{:S(2)}) %collective-permute-start.5) | collective-permute-done | bytes 8224 | tf_op jit(solution)/shard_map/ppermute | solution.py:369
  64.1 28.4 %force.2.own = f32[7,2,2,4,128]{4,3,2,1,0:T(4,128)S(1)} custom-call(f32[7,2,2,4,128]{4,3,2,1,0:T(4,128)S(1)} %pad_maximum_fusion.4.own, f32[7,2,2,4,128]{4,3,2,1,0:T(4,128)S(1)} %collective-permute-done.slab_a.a, f32[7,2,2,4,128]{4,3,2,1,0:T(4,128)S(1)} %collective-permute-done.1.slab_b.b, f32[7,6,4,128]{3,2,1,0:T(4,128)S(1)} %collective-permute-done.2.col_a.c, ...), custom_call_target="tpu_custom_call" | custom-call | tf_op jit(solution)/shard_map/force/pallas_call | solution.py:346
  92.5 4.2 %collective-permute-start.7 = (f32[7,2,2,4,128]{4,3,2,1,0:T(4,128)S(1)}, f32[7,2,2,4,128]{4,3,2,1,0:T(4,128)S(1)}, u32[]{:S(2)}, u32[]{:S(2)}) collective-permute-start(f32[7,2,2,4,128]{4,3,2,1,0:T(4,128)S(1)} %force.2.own), channel_id=1, source_target_pairs={{4,8},{8,4},{12,16},{16,12},{20,24},{24,20},{28,32},{32,28},{36,40... | collective-permute-start | bytes 172040 | tf_op jit(solution)/shard_map/ppermute | solution.py:369
  96.7 1.9 %collective-permute-start.6 = (f32[7,2,2,4,128]{4,3,2,1,0:T(4,128)S(1)}, f32[7,2,2,4,128]{4,3,2,1,0:T(4,128)S(1)}, u32[]{:S(2)}, u32[]{:S(2)}) collective-permute-start(f32[7,2,2,4,128]{4,3,2,1,0:T(4,128)S(1)} %force.2.own), channel_id=1, source_target_pairs={{0,4},{4,0},{8,12},{12,8},{16,20},{20,16},{24,28},{28,24},{32,36},... | collective-permute-start | bytes 172040 | tf_op jit(solution)/shard_map/ppermute | solution.py:364
  98.7 4.1 %collective-permute-done.7.slab_b = f32[7,2,2,4,128]{4,3,2,1,0:T(4,128)S(1)} collective-permute-done((f32[7,2,2,4,128]{4,3,2,1,0:T(4,128)S(1)}, f32[7,2,2,4,128]{4,3,2,1,0:T(4,128)S(1)}, u32[]{:S(2)}, u32[]{:S(2)}) %collective-permute-start.7) | collective-permute-done | bytes 57376 | tf_op jit(solution)/shard_map/ppermute | solution.py:369
  102.8 0.0 collective-permute-done.6.slab_a
  102.9 1.9 %collective-permute-start.8 = (f32[7,6,4,128]{3,2,1,0:T(4,128)S(1)}, f32[7,6,4,128]{3,2,1,0:T(4,128)S(1)}, u32[]{:S(2)}, u32[]{:S(2)}) collective-permute-start(f32[7,6,4,128]{3,2,1,0:T(4,128)S(1)} %pad_maximum_fusion.2), channel_id=1, source_target_pairs={{0,1},{1,0},{2,3},{3,2},{4,5},{5,4},{6,7},{7,6},{8,9},{9,8},{10,11... | collective-permute-start | bytes 258056 | tf_op jit(solution)/shard_map/ppermute | solution.py:364
  104.8 1.9 %collective-permute-start.9 = (f32[7,6,4,128]{3,2,1,0:T(4,128)S(1)}, f32[7,6,4,128]{3,2,1,0:T(4,128)S(1)}, u32[]{:S(2)}, u32[]{:S(2)}) collective-permute-start(f32[7,6,4,128]{3,2,1,0:T(4,128)S(1)} %pad_maximum_fusion.3), channel_id=1, source_target_pairs={{1,2},{2,1},{5,6},{6,5},{9,10},{10,9},{13,14},{14,13},{17,18},{18,... | collective-permute-start | bytes 258056 | tf_op jit(solution)/shard_map/ppermute | solution.py:369
  106.8 0.0 collective-permute-done.8.col_a
  106.8 5.4 %collective-permute-done.9.col_b = f32[7,6,4,128]{3,2,1,0:T(4,128)S(1)} collective-permute-done((f32[7,6,4,128]{3,2,1,0:T(4,128)S(1)}, f32[7,6,4,128]{3,2,1,0:T(4,128)S(1)}, u32[]{:S(2)}, u32[]{:S(2)}) %collective-permute-start.9) | collective-permute-done | bytes 86048 | tf_op jit(solution)/shard_map/ppermute | solution.py:369
  112.1 24.4 %density.3 = (f32[4,2,4,128]{3,2,1,0:T(4,128)S(1)}, f32[4,4,128]{2,1,0:T(4,128)S(1)}, f32[4,4,128]{2,1,0:T(4,128)S(1)}) custom-call(f32[7,2,2,4,128]{4,3,2,1,0:T(4,128)S(1)} %force.2.own, f32[7,2,2,4,128]{4,3,2,1,0:T(4,128)S(1)} %collective-permute-done.6.slab_a, f32[7,2,2,4,128]{4,3,2,1,0:T(4,128)S(1)} %collective-permute-done.7.slab_b, ...), custom_call_target="tpu_custom_call" | custom-call | tf_op jit(solution)/shard_map/density/pallas_call | solution.py:328
  136.6 1.9 %collective-permute-start.10 = (f32[4,4,128]{2,1,0:T(4,128)S(1)}, f32[4,4,128]{2,1,0:T(4,128)S(1)}, u32[]{:S(2)}, u32[]{:S(2)}) collective-permute-start(f32[4,4,128]{2,1,0:T(4,128)S(1)} %get-tuple-element.15), channel_id=1, source_target_pairs={{0,1},{1,0},{2,3},{3,2},{4,5},{5,4},{6,7},{7,6},{8,9},{9,8},{10,11... | collective-permute-start | bytes 24584 | tf_op jit(solution)/shard_map/ppermute | solution.py:364
  138.5 2.1 %collective-permute-start.11 = (f32[4,4,128]{2,1,0:T(4,128)S(1)}, f32[4,4,128]{2,1,0:T(4,128)S(1)}, u32[]{:S(2)}, u32[]{:S(2)}) collective-permute-start(f32[4,4,128]{2,1,0:T(4,128)S(1)} %get-tuple-element.16), channel_id=1, source_target_pairs={{1,2},{2,1},{5,6},{6,5},{9,10},{10,9},{13,14},{14,13},{17,18},{18,... | collective-permute-start | bytes 24584 | tf_op jit(solution)/shard_map/ppermute | solution.py:369
  140.6 0.6 slice.3
  141.2 0.0 collective-permute-done.10.rho_a
  141.2 3.8 %collective-permute-done.11.rho_b = f32[4,4,128]{2,1,0:T(4,128)S(1)} collective-permute-done((f32[4,4,128]{2,1,0:T(4,128)S(1)}, f32[4,4,128]{2,1,0:T(4,128)S(1)}, u32[]{:S(2)}, u32[]{:S(2)}) %collective-permute-start.11) | collective-permute-done | bytes 8224 | tf_op jit(solution)/shard_map/ppermute | solution.py:369
  145.0 29.0 %force.3 = (f32[3,2,2,4,128]{4,3,2,1,0:T(4,128)}, f32[3,2,2,4,128]{4,3,2,1,0:T(4,128)}) custom-call(f32[7,2,2,4,128]{4,3,2,1,0:T(4,128)S(1)} %force.2.own, f32[7,2,2,4,128]{4,3,2,1,0:T(4,128)S(1)} %collective-permute-done.6.slab_a, f32[7,2,2,4,128]{4,3,2,1,0:T(4,128)S(1)} %collective-permute-done.7.slab_b, ...), custom_call_target="tpu_custom_call" | custom-call | tf_op jit(solution)/shard_map/force/pallas_call | solution.py:346
  (10 shorter events, 0.2 us)
Async XLA Ops:
  2.2 15.9 %collective-permute-start.1 = (f32[7,2,2,4,128]{4,3,2,1,0:T(4,128)S(1)}, f32[7,2,2,4,128]{4,3,2,1,0:T(4,128)S(1)}, u32[]{:S(2)}, u32[]{:S(2)}) collective-permute-start(f32[7,2,2,4,128]{4,3,2,1,0:T(4,128)S(1)} %pad_maximum_fusion.4.own), channel_id=1, source_target_pairs={{4,8},{8,4},{12,16},{16,12},{20,24},{24,20},{28,32},{32,28},{36,40... | collective-permute-start | bytes 172040 | tf_op jit(solution)/shard_map/ppermute | solution.py:369
  15.9 6.1 %collective-permute-start = (f32[7,2,2,4,128]{4,3,2,1,0:T(4,128)S(1)}, f32[7,2,2,4,128]{4,3,2,1,0:T(4,128)S(1)}, u32[]{:S(2)}, u32[]{:S(2)}) collective-permute-start(f32[7,2,2,4,128]{4,3,2,1,0:T(4,128)S(1)} %pad_maximum_fusion.4.own), channel_id=1, source_target_pairs={{0,4},{4,0},{8,12},{12,8},{16,20},{20,16},{24,28},{28,24},{32,36},... | collective-permute-start | bytes 172040 | tf_op jit(solution)/shard_map/ppermute | solution.py:364
  22.1 4.9 %collective-permute-start.2 = (f32[7,6,4,128]{3,2,1,0:T(4,128)S(1)}, f32[7,6,4,128]{3,2,1,0:T(4,128)S(1)}, u32[]{:S(2)}, u32[]{:S(2)}) collective-permute-start(f32[7,6,4,128]{3,2,1,0:T(4,128)S(1)} %pad_maximum_fusion), channel_id=1, source_target_pairs={{0,1},{1,0},{2,3},{3,2},{4,5},{5,4},{6,7},{7,6},{8,9},{9,8},{10,11... | collective-permute-start | bytes 258056 | tf_op jit(solution)/shard_map/ppermute | solution.py:364
  24.0 7.3 %collective-permute-start.3 = (f32[7,6,4,128]{3,2,1,0:T(4,128)S(1)}, f32[7,6,4,128]{3,2,1,0:T(4,128)S(1)}, u32[]{:S(2)}, u32[]{:S(2)}) collective-permute-start(f32[7,6,4,128]{3,2,1,0:T(4,128)S(1)} %pad_maximum_fusion.1), channel_id=1, source_target_pairs={{1,2},{2,1},{5,6},{6,5},{9,10},{10,9},{13,14},{14,13},{17,18},{18,... | collective-permute-start | bytes 258056 | tf_op jit(solution)/shard_map/ppermute | solution.py:369
  55.7 4.9 %collective-permute-start.4 = (f32[4,4,128]{2,1,0:T(4,128)S(1)}, f32[4,4,128]{2,1,0:T(4,128)S(1)}, u32[]{:S(2)}, u32[]{:S(2)}) collective-permute-start(f32[4,4,128]{2,1,0:T(4,128)S(1)} %get-tuple-element.12), channel_id=1, source_target_pairs={{0,1},{1,0},{2,3},{3,2},{4,5},{5,4},{6,7},{7,6},{8,9},{9,8},{10,11... | collective-permute-start | bytes 24584 | tf_op jit(solution)/shard_map/ppermute | solution.py:364
  57.7 6.5 %collective-permute-start.5 = (f32[4,4,128]{2,1,0:T(4,128)S(1)}, f32[4,4,128]{2,1,0:T(4,128)S(1)}, u32[]{:S(2)}, u32[]{:S(2)}) collective-permute-start(f32[4,4,128]{2,1,0:T(4,128)S(1)} %get-tuple-element.13), channel_id=1, source_target_pairs={{1,2},{2,1},{5,6},{6,5},{9,10},{10,9},{13,14},{14,13},{17,18},{18,... | collective-permute-start | bytes 24584 | tf_op jit(solution)/shard_map/ppermute | solution.py:369
  92.5 10.3 %collective-permute-start.7 = (f32[7,2,2,4,128]{4,3,2,1,0:T(4,128)S(1)}, f32[7,2,2,4,128]{4,3,2,1,0:T(4,128)S(1)}, u32[]{:S(2)}, u32[]{:S(2)}) collective-permute-start(f32[7,2,2,4,128]{4,3,2,1,0:T(4,128)S(1)} %force.2.own), channel_id=1, source_target_pairs={{4,8},{8,4},{12,16},{16,12},{20,24},{24,20},{28,32},{32,28},{36,40... | collective-permute-start | bytes 172040 | tf_op jit(solution)/shard_map/ppermute | solution.py:369
  96.7 6.1 %collective-permute-start.6 = (f32[7,2,2,4,128]{4,3,2,1,0:T(4,128)S(1)}, f32[7,2,2,4,128]{4,3,2,1,0:T(4,128)S(1)}, u32[]{:S(2)}, u32[]{:S(2)}) collective-permute-start(f32[7,2,2,4,128]{4,3,2,1,0:T(4,128)S(1)} %force.2.own), channel_id=1, source_target_pairs={{0,4},{4,0},{8,12},{12,8},{16,20},{20,16},{24,28},{28,24},{32,36},... | collective-permute-start | bytes 172040 | tf_op jit(solution)/shard_map/ppermute | solution.py:364
  102.9 3.9 %collective-permute-start.8 = (f32[7,6,4,128]{3,2,1,0:T(4,128)S(1)}, f32[7,6,4,128]{3,2,1,0:T(4,128)S(1)}, u32[]{:S(2)}, u32[]{:S(2)}) collective-permute-start(f32[7,6,4,128]{3,2,1,0:T(4,128)S(1)} %pad_maximum_fusion.2), channel_id=1, source_target_pairs={{0,1},{1,0},{2,3},{3,2},{4,5},{5,4},{6,7},{7,6},{8,9},{9,8},{10,11... | collective-permute-start | bytes 258056 | tf_op jit(solution)/shard_map/ppermute | solution.py:364
  104.8 7.3 %collective-permute-start.9 = (f32[7,6,4,128]{3,2,1,0:T(4,128)S(1)}, f32[7,6,4,128]{3,2,1,0:T(4,128)S(1)}, u32[]{:S(2)}, u32[]{:S(2)}) collective-permute-start(f32[7,6,4,128]{3,2,1,0:T(4,128)S(1)} %pad_maximum_fusion.3), channel_id=1, source_target_pairs={{1,2},{2,1},{5,6},{6,5},{9,10},{10,9},{13,14},{14,13},{17,18},{18,... | collective-permute-start | bytes 258056 | tf_op jit(solution)/shard_map/ppermute | solution.py:369
  136.6 4.6 %collective-permute-start.10 = (f32[4,4,128]{2,1,0:T(4,128)S(1)}, f32[4,4,128]{2,1,0:T(4,128)S(1)}, u32[]{:S(2)}, u32[]{:S(2)}) collective-permute-start(f32[4,4,128]{2,1,0:T(4,128)S(1)} %get-tuple-element.15), channel_id=1, source_target_pairs={{0,1},{1,0},{2,3},{3,2},{4,5},{5,4},{6,7},{7,6},{8,9},{9,8},{10,11... | collective-permute-start | bytes 24584 | tf_op jit(solution)/shard_map/ppermute | solution.py:364
  138.5 6.5 %collective-permute-start.11 = (f32[4,4,128]{2,1,0:T(4,128)S(1)}, f32[4,4,128]{2,1,0:T(4,128)S(1)}, u32[]{:S(2)}, u32[]{:S(2)}) collective-permute-start(f32[4,4,128]{2,1,0:T(4,128)S(1)} %get-tuple-element.16), channel_id=1, source_target_pairs={{1,2},{2,1},{5,6},{6,5},{9,10},{10,9},{13,14},{14,13},{17,18},{18,... | collective-permute-start | bytes 24584 | tf_op jit(solution)/shard_map/ppermute | solution.py:369

commit v3 on v2

v3 whole, which is shorter than its diff:
```python
import functools
import math

import jax
import jax.numpy as jnp
from jax import lax
from jax.experimental import pallas as pl
from jax.experimental.pallas import tpu as pltpu
from jax.sharding import PartitionSpec as P

STEPS = 2
SLOTS = 128
MASS = 8.0 / SLOTS
KERNEL_NORM = 21.0 / (16.0 * math.pi)
TAIT = 10.0 * 10.0 / 7.0
TIME_STEP = 0.02
GRAVITY = 1.0
FAR = 1000.0
TINY = 1e-30

PARTS_J = (0, 0, 1, 1, 0, 2)
PARTS_I = (0, 1, 0, 1, 2, 0)
ROW_X = 0
ROW_NJ = 18
ROW_ONE = 21
ROW_RHO = 24
ROW_P = 27
ROW_V = 32
ROW_WJ = 50
SHORT = 32
LONG = 64
DEPTH = 128
SUM_ROWS = ((ROW_X, ROW_X + 2, ROW_X + 5), (ROW_X + 6, ROW_X + 8, ROW_X + 11), (ROW_X + 12, ROW_X + 14, ROW_X + 17))


def split3(value):
    high = value.astype(jnp.bfloat16).astype(jnp.float32)
    rest = value - high
    middle = rest.astype(jnp.bfloat16).astype(jnp.float32)
    return (high, middle, rest - middle)


def dot(lhs, rhs):
    return jnp.dot(lhs, rhs, preferred_element_type=jnp.float32)


def fold(tile):
    return jnp.sum(tile.reshape(tile.shape[0] // 8, 8, tile.shape[1]), axis=0)


def parities():
    return lax.axis_index("slab") % 2 == 0, lax.axis_index("col") % 2 == 0


def column_of(refs, comp, ix, iy):
    own, slab_a, slab_b, *cols = refs
    slab_even, col_even = parities()
    if iy in (0, 3):
        col_a, col_b = cols
        near, other = (col_b, col_a) if iy == 0 else (col_a, col_b)
        rows = lambda at: jnp.where(col_even, near[comp, at], other[comp, at])
        if 2 <= ix < 4:
            return rows(ix)
        at_a, at_b = ix % 2, 4 + ix % 2
        first, second = (at_b, at_a) if ix < 2 else (at_a, at_b)
        return jnp.where(slab_even, rows(first), rows(second))
    if 2 <= ix < 4:
        return own[comp, ix - 2, iy - 1]
    first, second = (slab_b, slab_a) if ix < 2 else (slab_a, slab_b)
    return jnp.where(slab_even, first[comp, ix % 2, iy - 1], second[comp, ix % 2, iy - 1])


def centred(refs, ix, iy):
    places = []
    for axis in range(3):
        half = 0.5 * column_of(refs, axis, ix, iy)
        if axis == 2:
            shift = lax.broadcasted_iota(jnp.int32, half.shape, 0).astype(jnp.float32) - 0.5 * half.shape[0]
        else:
            shift = (ix - 3.0, iy - 2.0)[axis]
        places.append(half + shift)
    return places


def source_rows(refs, ix, iy, with_velocity):
    live = column_of(refs, 6, ix, iy) > 0.5
    places = [jnp.where(live, place, FAR) for place in centred(refs, ix, iy)]
    rows = {}
    for axis in range(3):
        parts = split3(places[axis])
        for at, part in enumerate(PARTS_J):
            rows[ROW_X + 6 * axis + at] = parts[part]
    norm = places[0] * places[0] + places[1] * places[1] + places[2] * places[2]
    for at, part in enumerate(split3(norm)):
        rows[ROW_NJ + at] = part
        rows[ROW_ONE + at] = jnp.ones_like(part)
    if with_velocity:
        speeds = [column_of(refs, 3 + axis, ix, iy) for axis in range(3)]
        along = 0.0
        for axis in range(3):
            parts = split3(speeds[axis])
            for at, part in enumerate(PARTS_J):
                rows[ROW_V + 6 * axis + at] = parts[part]
            along = along + speeds[axis] * places[axis]
        for at, part in enumerate(split3(along)):
            rows[ROW_WJ + at] = part
    return rows


def put_rows(table, column, rows, depth):
    blank = jnp.zeros((table.shape[1], SLOTS), jnp.float32)
    for row in range(depth):
        table[column, :, row, :] = rows.get(row, blank)


def turned_cell(table, column, z):
    rows = table[column, z]
    flat = jnp.transpose(rows)
    return jnp.concatenate([flat, jnp.zeros((SLOTS, DEPTH - rows.shape[0]), jnp.float32)], axis=1).astype(jnp.bfloat16)


def deep(rows):
    return jnp.concatenate([rows, jnp.zeros((DEPTH - rows.shape[0], SLOTS), jnp.float32)], axis=0).astype(jnp.bfloat16)


def gap_rows_of(places):
    rows = {}
    for axis in range(3):
        parts = split3(-2.0 * places[axis])
        for at, part in enumerate(PARTS_I):
            rows[ROW_X + 6 * axis + at] = parts[part]
    norm = places[0] * places[0] + places[1] * places[1] + places[2] * places[2]
    for at, part in enumerate(split3(norm)):
        rows[ROW_NJ + at] = jnp.ones_like(part)
        rows[ROW_ONE + at] = part
    return rows


def closing_rows_of(places, speeds):
    rows = {}
    along = 0.0
    for axis in range(3):
        place_parts = split3(2.0 * places[axis])
        speed_parts = split3(2.0 * speeds[axis])
        for at, part in enumerate(PARTS_I):
            rows[ROW_X + 6 * axis + at] = speed_parts[part]
            rows[ROW_V + 6 * axis + at] = place_parts[part]
        along = along + places[axis] * speeds[axis]
    for at, part in enumerate(split3(-2.0 * along)):
        rows[ROW_WJ + at] = jnp.full_like(part, -2.0)
        rows[ROW_ONE + at] = part
    return rows


def sum_rows_of(value, row):
    rows = {}
    for at, part in enumerate(split3(value)):
        rows[row + at] = jnp.ones_like(part)
        rows[ROW_ONE + at] = part
    return rows


def source_ys(inner):
    return (1, 2) if inner else (0, 3)


def source_columns(inner, tx, ty):
    return [(tx + dx) * 2 + (at if inner else ty) for dx in range(3) for at in range(2 if inner else 1)]


def density_kernel(inner, refs, partial, rho_ref, table, turned, weights):
    cells_z = refs[0].shape[3]
    for ix in range(6):
        for at, iy in enumerate(source_ys(inner)):
            put_rows(table, ix * 2 + at, source_rows(refs, ix, iy, False), SHORT)

    def turn(column, carry):
        for z in range(cells_z):
            turned[column, z] = turned_cell(table, column, z)
        return carry

    lax.fori_loop(0, 12, turn, 0)
    for tx in range(4):
        for ty in range(2):
            places = centred(refs, tx + 1, ty + 1)
            put_rows(weights, tx * 2 + ty, gap_rows_of(places), SHORT)

    def target(step, carry):
        tx, ty = step // 2, step % 2
        for pair in range(cells_z // 2):
            rhs = jnp.concatenate([deep(weights[step, 2 * pair]), deep(weights[step, 2 * pair + 1])], axis=1)
            zero = jnp.zeros((8, SLOTS), jnp.float32)
            fourths, fifths = [zero, zero], [zero, zero]
            for column in source_columns(inner, tx, ty):
                for z in range(max(0, 2 * pair - 1), min(cells_z, 2 * pair + 3)):
                    gap = dot(turned[column, z], rhs)
                    for half in range(2):
                        if abs(2 * pair + half - z) > 1:
                            continue
                        near = jnp.maximum(gap[:, half * SLOTS : (half + 1) * SLOTS], TINY)
                        inside = jnp.maximum(1.0 - 1.0 / lax.rsqrt(near), 0.0)
                        square = inside * inside
                        fourth = square * square
                        fourths[half] = fourths[half] + fold(fourth)
                        fifths[half] = fifths[half] + fold(fourth * inside)
            for half in range(2):
                total = 5.0 * fourths[half] - 4.0 * fifths[half]
                row = pl.ds(2 * pair + half, 1)
                total = (MASS * KERNEL_NORM) * jnp.sum(total, axis=0, keepdims=True)
                if partial is not None:
                    total = total + partial[tx, ty, row, :]
                rho_ref[tx, ty, row, :] = total
        return carry

    lax.fori_loop(0, 8, target, 0)


def inner_density_kernel(own, slab_a, slab_b, rho_ref, *scratch):
    density_kernel(True, (own, slab_a, slab_b), None, rho_ref, *scratch)


def outer_density_kernel(own, slab_a, slab_b, col_a, col_b, partial, rho_ref, send_a, send_b, *scratch):
    density_kernel(False, (own, slab_a, slab_b, col_a, col_b), partial, rho_ref, *scratch)
    for ix in range(2):
        for iy in range(2):
            rho_ref[ix + 1, iy] = rho_ref[ix + 1, iy] + (1.0 - own[6, ix, iy]) * (MASS * KERNEL_NORM)
    col_even = parities()[1]
    for ix in range(4):
        low, high = rho_ref[ix, 0], rho_ref[ix, 1]
        send_a[ix] = jnp.where(col_even, high, low)
        send_b[ix] = jnp.where(col_even, low, high)


def pressure_ratio(density):
    cubed = density * density * density
    return TAIT * (cubed * cubed * density - 1.0) / (density * density)


def force_kernel(inner, refs, rho, rho_a, rho_b, store, table, turned, weights, long_weights, spread):
    cells_z = refs[0].shape[3]
    col_even = parities()[1]
    for ix in range(4):
        for side, iy in enumerate(source_ys(inner)):
            rows = source_rows(refs, ix + 1, iy, True)
            if iy == 0:
                density = jnp.where(col_even, rho_b[ix], rho_a[ix])
            elif iy == 3:
                density = jnp.where(col_even, rho_a[ix], rho_b[ix])
            else:
                density = rho[ix, iy - 1]
            density = jnp.maximum(density, MASS * KERNEL_NORM)
            for at, part in enumerate(split3(density)):
                rows[ROW_RHO + at] = part
            for at, part in enumerate(split3(pressure_ratio(density))):
                rows[ROW_P + at] = part
            put_rows(table, ix * 2 + side, rows, LONG)

    at_row = lax.broadcasted_iota(jnp.int32, (DEPTH, SLOTS), 0)
    picks = []
    for rows in SUM_ROWS:
        chosen = (at_row == rows[0]) | (at_row == rows[1]) | (at_row == rows[2])
        picks.append(jnp.where(chosen, 1.0, 0.0).astype(jnp.bfloat16))
    picks = jnp.concatenate(picks, axis=1)

    def turn(column, carry):
        flats = [turned_cell(table, column, z) for z in range(cells_z)]
        for z in range(cells_z):
            turned[column, z] = flats[z]
        values = dot(jnp.concatenate(flats, axis=0), picks)
        for z in range(cells_z):
            spread[column, z] = values[z * SLOTS : (z + 1) * SLOTS]
        return carry

    lax.fori_loop(0, 8, turn, 0)

    for tx in range(2):
        for ty in range(2):
            places = centred(refs, tx + 2, ty + 1)
            speeds = [column_of(refs, 3 + axis, tx + 2, ty + 1) for axis in range(3)]
            density = jnp.maximum(rho[tx + 1, ty], MASS * KERNEL_NORM)
            put_rows(weights.at[0], tx * 2 + ty, gap_rows_of(places), SHORT)
            put_rows(weights.at[1], tx * 2 + ty, sum_rows_of(density, ROW_RHO), SHORT)
            put_rows(weights.at[2], tx * 2 + ty, sum_rows_of(pressure_ratio(density), ROW_P), SHORT)
            put_rows(long_weights, tx * 2 + ty, closing_rows_of(places, speeds), LONG)

    def target(step, carry):
        tx, ty = step // 2, step % 2
        for zt in range(cells_z):
            rhs = jnp.concatenate([deep(weights[0, step, zt]), deep(long_weights[step, zt])], axis=1)
            rhs_sums = jnp.concatenate([deep(weights[1, step, zt]), deep(weights[2, step, zt])], axis=1)
            sums = [jnp.zeros((8, SLOTS), jnp.float32)] * 4
            for column in source_columns(inner, tx, ty):
                for z in range(max(0, zt - 1), min(cells_z, zt + 2)):
                    both = dot(turned[column, z], rhs)
                    pair_sums = dot(turned[column, z], rhs_sums)
                    near = jnp.maximum(both[:, :SLOTS], TINY)
                    inside = jnp.maximum(1.0 - near * lax.rsqrt(near), 0.0)
                    closing = jnp.maximum(both[:, SLOTS:], 0.0)
                    below = (near + 0.0025) * pair_sums[:, :SLOTS]
                    strength = pair_sums[:, SLOTS:] + closing / below
                    strength = strength * (inside * inside * inside)
                    for axis in range(3):
                        place = spread[column, z, :, axis * SLOTS : (axis + 1) * SLOTS]
                        sums[axis] = sums[axis] + fold(strength * place)
                    sums[3] = sums[3] + fold(strength)
            store(tx, ty, zt, [jnp.sum(total, axis=0, keepdims=True) for total in sums])
        return carry

    lax.fori_loop(0, 4, target, 0)


def inner_force_kernel(own, slab_a, slab_b, rho, sums_ref, *scratch):
    def store(tx, ty, zt, sums):
        for at in range(4):
            sums_ref[at, tx, ty, pl.ds(zt, 1), :] = sums[at]

    force_kernel(True, (own, slab_a, slab_b), rho, None, None, store, *scratch)


def outer_force_kernel(last, own, slab_a, slab_b, col_a, col_b, rho, rho_a, rho_b, partial, *outs_and_scratch):
    outs, scratch = outs_and_scratch[: 2 if last else 1], outs_and_scratch[2 if last else 1 :]

    def store(tx, ty, zt, sums):
        row = pl.ds(zt, 1)
        *parts, whole = [sums[at] + partial[at, tx, ty, row, :] for at in range(4)]
        live = own[6, tx, ty, row, :] > 0.5
        for axis in range(3):
            old_place = own[axis, tx, ty, row, :]
            old_speed = own[3 + axis, tx, ty, row, :]
            shift = zt - 0.5 * own.shape[3]
            if axis < 2:
                shift = jnp.asarray((tx, ty)[axis] - 1, jnp.int32).astype(jnp.float32)
            place = 0.5 * old_place + shift
            pull = (10.0 * KERNEL_NORM * MASS) * (place * whole - parts[axis])
            if axis == 2:
                pull = pull - GRAVITY
            speed = old_speed + TIME_STEP * pull
            new_place = jnp.where(live, old_place + TIME_STEP * speed, old_place)
            new_speed = jnp.where(live, speed, old_speed)
            if last:
                outs[0][axis, tx, ty, row, :] = new_place
                outs[1][axis, tx, ty, row, :] = new_speed
            else:
                outs[0][axis, tx, ty, row, :] = new_place
                outs[0][3 + axis, tx, ty, row, :] = new_speed
        if not last:
            outs[0][6, tx, ty, row, :] = own[6, tx, ty, row, :]

    force_kernel(False, (own, slab_a, slab_b, col_a, col_b), rho, rho_a, rho_b, store, *scratch)


VMEM_SPEC = pl.BlockSpec(memory_space=pltpu.VMEM)
INNER_WORK = 1 << 34
OUTER_WORK = 1 << 33


def shaped(*shape):
    return jax.ShapeDtypeStruct(shape, jnp.float32)


def call(kernel, name, work, outs, scratch, *operands):
    return pl.pallas_call(
        kernel,
        name=name,
        out_shape=outs,
        in_specs=[VMEM_SPEC] * len(operands),
        out_specs=jax.tree.map(lambda _: VMEM_SPEC, outs),
        scratch_shapes=scratch,
        cost_estimate=pl.CostEstimate(flops=work, bytes_accessed=1 << 19, transcendentals=0),
        compiler_params=pltpu.CompilerParams(vmem_limit_bytes=32 << 20),
    )(*operands)


def densities(inner, state, *halo):
    cells_z = state.shape[3]
    scratch = [
        pltpu.VMEM((12, cells_z, SHORT, SLOTS), jnp.float32),
        pltpu.VMEM((12, cells_z, SLOTS, DEPTH), jnp.bfloat16),
        pltpu.VMEM((8, cells_z, SHORT, SLOTS), jnp.float32),
    ]
    whole, edge = shaped(4, 2, cells_z, SLOTS), shaped(4, cells_z, SLOTS)
    if inner:
        return call(inner_density_kernel, "inner_density", INNER_WORK, whole, scratch, state, *halo)
    return call(outer_density_kernel, "outer_density", OUTER_WORK, (whole, edge, edge), scratch, state, *halo)


def forces(inner, last, state, *halo):
    cells_z = state.shape[3]
    block = state.shape[1:]
    scratch = [
        pltpu.VMEM((8, cells_z, LONG, SLOTS), jnp.float32),
        pltpu.VMEM((8, cells_z, SLOTS, DEPTH), jnp.bfloat16),
        pltpu.VMEM((3, 4, cells_z, SHORT, SLOTS), jnp.float32),
        pltpu.VMEM((4, cells_z, LONG, SLOTS), jnp.float32),
        pltpu.VMEM((8, cells_z, SLOTS, 3 * SLOTS), jnp.float32),
    ]
    if inner:
        return call(inner_force_kernel, "inner_force", INNER_WORK, shaped(4, *block), scratch, state, *halo)
    outs = (shaped(3, *block), shaped(3, *block)) if last else shaped(7, *block)
    return call(functools.partial(outer_force_kernel, last), "outer_force", OUTER_WORK, outs, scratch, state, *halo)


def swap_even(value, axis):
    return lax.ppermute(value, axis, [(i, i ^ 1) for i in range(lax.axis_size(axis))])


def swap_odd(value, axis):
    count = lax.axis_size(axis)
    return lax.ppermute(value, axis, [(i, i - 1 if i % 2 == 0 else i + 1) for i in range(1, count - 1)])


def per_device(offsets, velocity, occupancy):
    slot_rank = jnp.arange(SLOTS, dtype=jnp.int32)
    live = (slot_rank < occupancy[..., None]).astype(jnp.float32)
    state = jnp.concatenate([offsets, velocity, live[None]], axis=0)
    col_odd = lax.axis_index("col") % 2
    for section in range(STEPS):
        slab_b, slab_a = swap_odd(state, "slab"), swap_even(state, "slab")
        edges = [
            jnp.concatenate([lax.dynamic_index_in_dim(part, y, 2, keepdims=False) for part in (slab_a, state, slab_b)], axis=1)
            for y in (col_odd, 1 - col_odd)
        ]
        col_b, col_a = swap_odd(edges[0], "col"), swap_even(edges[1], "col")
        rho = densities(True, state, slab_a, slab_b)
        rho, rho_a, rho_b = densities(False, state, slab_a, slab_b, col_a, col_b, rho)
        rho_b, rho_a = swap_odd(rho_b, "col"), swap_even(rho_a, "col")
        sums = forces(True, False, state, slab_a, slab_b, rho)
        last = section == STEPS - 1
        state = forces(False, last, state, slab_a, slab_b, col_a, col_b, rho, rho_a, rho_b, sums)
    return (state[0], state[1], rho[1:3])


def solution(mesh):
    placed = P(None, "slab", "col", None, None)
    return jax.shard_map(
        per_device,
        mesh=mesh,
        in_specs=(placed, placed, P("slab", "col", None)),
        out_specs=(placed, placed, P("slab", "col", None, None)),
        check_vma=False,
    )
```

time: 174 us -> 157 us (0.902)
  waiting for transfers between devices: 25.2 us -> 8.21 us
  starting transfers between devices: 39.4 us -> 44 us
  Pallas kernels: 106 us -> 102 us
    ppermute x6, waiting for transfers between devices: 21.2 us -> 4.25 us  [swap_odd(): lax.ppermute(value, axis, [(i, i - 1 if i % 2 == 0 else i + 1) for i in r...]
    ppermute x6, starting transfers between devices: 27.9 us -> 32.4 us  [swap_odd(): lax.ppermute(value, axis, [(i, i - 1 if i % 2 == 0 else i + 1) for i in r...]
    pallas_call x4 -> x8, Pallas kernels: 106 us -> 102 us  [call(): pl.pallas_call(kernel, name=name, out_shape=outs, in_specs=[VMEM_SPEC] *...]
  transfers between devices with their start and end apart: 12 -> 12, of which waited for: 7 -> 3; matrix products, arithmetic and copies ran while one was open for 0% -> 0% of each run, Pallas kernels for 0% -> 40%
where the time goes in v3:
time: 157 us
  Pallas kernels  102 us (65%)
  starting transfers between devices  44 us (28%)
  waiting for transfers between devices  8.21 us (5%)
  other arithmetic  1.61 us (1%)
    pallas_call x8, Pallas kernels, call(): pl.pallas_call(kernel, name=name, out_shape=outs, in_specs=[VMEM_SPEC] *...  102 us
    ppermute x6, starting transfers between devices, swap_odd(): lax.ppermute(value, axis, [(i, i - 1 if i % 2 == 0 else i + 1) for i in r...  32.4 us
    ppermute x6, starting transfers between devices, swap_even(): lax.ppermute(value, axis, [(i, i ^ 1) for i in range(lax.axis_size(axis))])  11.5 us
    ppermute x6, waiting for transfers between devices, swap_odd(): lax.ppermute(value, axis, [(i, i - 1 if i % 2 == 0 else i + 1) for i in r...  4.25 us
    ppermute x6, waiting for transfers between devices, swap_even(): lax.ppermute(value, axis, [(i, i ^ 1) for i in range(lax.axis_size(axis))])  3.96 us
  transfers between devices with their start and end apart: 12, of which 3 were waited for; matrix products, arithmetic and copies ran while one was open for 0% of the time, Pallas kernels for 40%

profile of v3, /device:TPU:24, one launch (start us, length us, event | category | flops | bytes accessed | tf_op | source)
XLA Modules:
  0.0 157.0 jit_solution(17359465510628358479)
XLA Ops:
  0.6 0.8 fusion
  1.4 0.8 pad_maximum_fusion.4.own
  2.2 13.8 %collective-permute-start.1 = (f32[7,2,2,4,128]{4,3,2,1,0:T(4,128)S(1)}, f32[7,2,2,4,128]{4,3,2,1,0:T(4,128)S(1)}, u32[]{:S(2)}, u32[]{:S(2)}) collective-permute-start(f32[7,2,2,4,128]{4,3,2,1,0:T(4,128)S(1)} %pad_maximum_fusion.4.own), channel_id=1, source_target_pairs={{4,8},{8,4},{12,16},{16,12},{20,24},{24,20},{28,32},{32,28},{36,40... | collective-permute-start | bytes 172040 | tf_op jit(solution)/shard_map/ppermute | solution.py:409
  15.9 1.9 %collective-permute-start = (f32[7,2,2,4,128]{4,3,2,1,0:T(4,128)S(1)}, f32[7,2,2,4,128]{4,3,2,1,0:T(4,128)S(1)}, u32[]{:S(2)}, u32[]{:S(2)}) collective-permute-start(f32[7,2,2,4,128]{4,3,2,1,0:T(4,128)S(1)} %pad_maximum_fusion.4.own), channel_id=1, source_target_pairs={{0,4},{4,0},{8,12},{12,8},{16,20},{20,16},{24,28},{28,24},{32,36},... | collective-permute-start | bytes 172040 | tf_op jit(solution)/shard_map/ppermute | solution.py:404
  17.9 0.2 collective-permute-done.1.slab_b
  18.1 3.9 %collective-permute-done.slab_a = f32[7,2,2,4,128]{4,3,2,1,0:T(4,128)S(1)} collective-permute-done((f32[7,2,2,4,128]{4,3,2,1,0:T(4,128)S(1)}, f32[7,2,2,4,128]{4,3,2,1,0:T(4,128)S(1)}, u32[]{:S(2)}, u32[]{:S(2)}) %collective-permute-start) | collective-permute-done | bytes 57376 | tf_op jit(solution)/shard_map/ppermute | solution.py:404
  22.1 1.9 %collective-permute-start.2 = (f32[7,6,4,128]{3,2,1,0:T(4,128)S(1)}, f32[7,6,4,128]{3,2,1,0:T(4,128)S(1)}, u32[]{:S(2)}, u32[]{:S(2)}) collective-permute-start(f32[7,6,4,128]{3,2,1,0:T(4,128)S(1)} %pad_maximum_fusion), channel_id=1, source_target_pairs={{0,1},{1,0},{2,3},{3,2},{4,5},{5,4},{6,7},{7,6},{8,9},{9,8},{10,11... | collective-permute-start | bytes 258056 | tf_op jit(solution)/shard_map/ppermute | solution.py:404
  24.0 3.0 %collective-permute-start.3 = (f32[7,6,4,128]{3,2,1,0:T(4,128)S(1)}, f32[7,6,4,128]{3,2,1,0:T(4,128)S(1)}, u32[]{:S(2)}, u32[]{:S(2)}) collective-permute-start(f32[7,6,4,128]{3,2,1,0:T(4,128)S(1)} %pad_maximum_fusion.1), channel_id=1, source_target_pairs={{1,2},{2,1},{5,6},{6,5},{9,10},{10,9},{13,14},{14,13},{17,18},{18,... | collective-permute-start | bytes 258056 | tf_op jit(solution)/shard_map/ppermute | solution.py:409
  27.0 15.2 %inner_density.2.partial = f32[4,2,4,128]{3,2,1,0:T(4,128)S(1)} custom-call(f32[7,2,2,4,128]{4,3,2,1,0:T(4,128)S(1)} %pad_maximum_fusion.4.own, f32[7,2,2,4,128]{4,3,2,1,0:T(4,128)S(1)} %collective-permute-done.slab_a, f32[7,2,2,4,128]{4,3,2,1,0:T(4,128)S(1)} %collective-permute-done.1.slab_b), custom_call_target="tpu_custom_call" | custom-call | flops 17179869184 | bytes 524288 | tf_op jit(solution)/shard_map/inner_density/pallas_call | solution.py:362
  42.2 0.0 collective-permute-done.2.col_a
  42.2 0.0 collective-permute-done.3.col_b
  42.2 9.2 %outer_density.2 = (f32[4,2,4,128]{3,2,1,0:T(4,128)S(1)}, f32[4,4,128]{2,1,0:T(4,128)S(1)}, f32[4,4,128]{2,1,0:T(4,128)S(1)}) custom-call(f32[7,2,2,4,128]{4,3,2,1,0:T(4,128)S(1)} %pad_maximum_fusion.4.own, f32[7,2,2,4,128]{4,3,2,1,0:T(4,128)S(1)} %collective-permute-done.slab_a, f32[7,2,2,4,128]{4,3,2,1,0:T(4,128)S(1)} %collective-permute-done.1.slab_b, ...), custom_call_target="tpu_custom_call" | custom-call | flops 8589934592 | bytes 524288 | tf_op jit(solution)/shard_map/outer_density/pallas_call | solution.py:362
  51.4 1.9 %collective-permute-start.4 = (f32[4,4,128]{2,1,0:T(4,128)S(1)}, f32[4,4,128]{2,1,0:T(4,128)S(1)}, u32[]{:S(2)}, u32[]{:S(2)}) collective-permute-start(f32[4,4,128]{2,1,0:T(4,128)S(1)} %get-tuple-element.12), channel_id=1, source_target_pairs={{0,1},{1,0},{2,3},{3,2},{4,5},{5,4},{6,7},{7,6},{8,9},{9,8},{10,11... | collective-permute-start | bytes 24584 | tf_op jit(solution)/shard_map/ppermute | solution.py:404
  53.3 4.2 %collective-permute-start.5 = (f32[4,4,128]{2,1,0:T(4,128)S(1)}, f32[4,4,128]{2,1,0:T(4,128)S(1)}, u32[]{:S(2)}, u32[]{:S(2)}) collective-permute-start(f32[4,4,128]{2,1,0:T(4,128)S(1)} %get-tuple-element.13), channel_id=1, source_target_pairs={{1,2},{2,1},{5,6},{6,5},{9,10},{10,9},{13,14},{14,13},{17,18},{18,... | collective-permute-start | bytes 24584 | tf_op jit(solution)/shard_map/ppermute | solution.py:409
  57.6 15.9 %inner_force.2.partial = f32[4,2,2,4,128]{4,3,2,1,0:T(4,128)S(1)} custom-call(f32[7,2,2,4,128]{4,3,2,1,0:T(4,128)S(1)} %pad_maximum_fusion.4.own, f32[7,2,2,4,128]{4,3,2,1,0:T(4,128)S(1)} %collective-permute-done.slab_a, f32[7,2,2,4,128]{4,3,2,1,0:T(4,128)S(1)} %collective-permute-done.1.slab_b, f32[4,2,4,128]{3,2,1,0:T(4,128)S(1)} %get-tuple-element.11.rho), custom_call_target="tpu_custom_call" | custom-call | flops 17179869184 | bytes 524288 | tf_op jit(solution)/shard_map/inner_force/pallas_call | solution.py:362
  73.5 0.0 collective-permute-done.5.rho_b
  73.5 10.2 %outer_force.2.own = f32[7,2,2,4,128]{4,3,2,1,0:T(4,128)S(1)} custom-call(f32[7,2,2,4,128]{4,3,2,1,0:T(4,128)S(1)} %pad_maximum_fusion.4.own, f32[7,2,2,4,128]{4,3,2,1,0:T(4,128)S(1)} %collective-permute-done.slab_a, f32[7,2,2,4,128]{4,3,2,1,0:T(4,128)S(1)} %collective-permute-done.1.slab_b, f32[7,6,4,128]{3,2,1,0:T(4,128)S(1)} %collective-permute-done.2.col_a, ...), custom_call_target="tpu_custom_call" | custom-call | flops 8589934592 | bytes 524288 | tf_op jit(solution)/shard_map/outer_force/pallas_call | solution.py:362
  83.7 4.3 %collective-permute-start.7 = (f32[7,2,2,4,128]{4,3,2,1,0:T(4,128)S(1)}, f32[7,2,2,4,128]{4,3,2,1,0:T(4,128)S(1)}, u32[]{:S(2)}, u32[]{:S(2)}) collective-permute-start(f32[7,2,2,4,128]{4,3,2,1,0:T(4,128)S(1)} %outer_force.2.own), channel_id=1, source_target_pairs={{4,8},{8,4},{12,16},{16,12},{20,24},{24,20},{28,32},{32,28},{36,40... | collective-permute-start | bytes 172040 | tf_op jit(solution)/shard_map/ppermute | solution.py:409
  88.0 1.9 %collective-permute-start.6 = (f32[7,2,2,4,128]{4,3,2,1,0:T(4,128)S(1)}, f32[7,2,2,4,128]{4,3,2,1,0:T(4,128)S(1)}, u32[]{:S(2)}, u32[]{:S(2)}) collective-permute-start(f32[7,2,2,4,128]{4,3,2,1,0:T(4,128)S(1)} %outer_force.2.own), channel_id=1, source_target_pairs={{0,4},{4,0},{8,12},{12,8},{16,20},{20,16},{24,28},{28,24},{32,36},... | collective-permute-start | bytes 172040 | tf_op jit(solution)/shard_map/ppermute | solution.py:404
  90.0 4.1 %collective-permute-done.7.slab_b = f32[7,2,2,4,128]{4,3,2,1,0:T(4,128)S(1)} collective-permute-done((f32[7,2,2,4,128]{4,3,2,1,0:T(4,128)S(1)}, f32[7,2,2,4,128]{4,3,2,1,0:T(4,128)S(1)}, u32[]{:S(2)}, u32[]{:S(2)}) %collective-permute-start.7) | collective-permute-done | bytes 57376 | tf_op jit(solution)/shard_map/ppermute | solution.py:409
  94.0 0.0 collective-permute-done.6.slab_a
  94.1 1.9 %collective-permute-start.8 = (f32[7,6,4,128]{3,2,1,0:T(4,128)S(1)}, f32[7,6,4,128]{3,2,1,0:T(4,128)S(1)}, u32[]{:S(2)}, u32[]{:S(2)}) collective-permute-start(f32[7,6,4,128]{3,2,1,0:T(4,128)S(1)} %pad_maximum_fusion.2), channel_id=1, source_target_pairs={{0,1},{1,0},{2,3},{3,2},{4,5},{5,4},{6,7},{7,6},{8,9},{9,8},{10,11... | collective-permute-start | bytes 258056 | tf_op jit(solution)/shard_map/ppermute | solution.py:404
  96.1 1.9 %collective-permute-start.9 = (f32[7,6,4,128]{3,2,1,0:T(4,128)S(1)}, f32[7,6,4,128]{3,2,1,0:T(4,128)S(1)}, u32[]{:S(2)}, u32[]{:S(2)}) collective-permute-start(f32[7,6,4,128]{3,2,1,0:T(4,128)S(1)} %pad_maximum_fusion.3), channel_id=1, source_target_pairs={{1,2},{2,1},{5,6},{6,5},{9,10},{10,9},{13,14},{14,13},{17,18},{18,... | collective-permute-start | bytes 258056 | tf_op jit(solution)/shard_map/ppermute | solution.py:409
  98.0 15.2 %inner_density.3.partial = f32[4,2,4,128]{3,2,1,0:T(4,128)S(1)} custom-call(f32[7,2,2,4,128]{4,3,2,1,0:T(4,128)S(1)} %outer_force.2.own, f32[7,2,2,4,128]{4,3,2,1,0:T(4,128)S(1)} %collective-permute-done.6.slab_a, f32[7,2,2,4,128]{4,3,2,1,0:T(4,128)S(1)} %collective-permute-done.7.slab_b), custom_call_target="tpu_custom_call" | custom-call | flops 17179869184 | bytes 524288 | tf_op jit(solution)/shard_map/inner_density/pallas_call | solution.py:362
  113.2 0.0 collective-permute-done.8.col_a
  113.2 0.0 collective-permute-done.9.col_b
  113.2 9.2 %outer_density.3 = (f32[4,2,4,128]{3,2,1,0:T(4,128)S(1)}, f32[4,4,128]{2,1,0:T(4,128)S(1)}, f32[4,4,128]{2,1,0:T(4,128)S(1)}) custom-call(f32[7,2,2,4,128]{4,3,2,1,0:T(4,128)S(1)} %outer_force.2.own, f32[7,2,2,4,128]{4,3,2,1,0:T(4,128)S(1)} %collective-permute-done.6.slab_a, f32[7,2,2,4,128]{4,3,2,1,0:T(4,128)S(1)} %collective-permute-done.7.slab_b, ...), custom_call_target="tpu_custom_call" | custom-call | flops 8589934592 | bytes 524288 | tf_op jit(solution)/shard_map/outer_density/pallas_call | solution.py:362
  122.4 1.9 %collective-permute-start.10 = (f32[4,4,128]{2,1,0:T(4,128)S(1)}, f32[4,4,128]{2,1,0:T(4,128)S(1)}, u32[]{:S(2)}, u32[]{:S(2)}) collective-permute-start(f32[4,4,128]{2,1,0:T(4,128)S(1)} %get-tuple-element.15), channel_id=1, source_target_pairs={{0,1},{1,0},{2,3},{3,2},{4,5},{5,4},{6,7},{7,6},{8,9},{9,8},{10,11... | collective-permute-start | bytes 24584 | tf_op jit(solution)/shard_map/ppermute | solution.py:404
  124.4 5.3 %collective-permute-start.11 = (f32[4,4,128]{2,1,0:T(4,128)S(1)}, f32[4,4,128]{2,1,0:T(4,128)S(1)}, u32[]{:S(2)}, u32[]{:S(2)}) collective-permute-start(f32[4,4,128]{2,1,0:T(4,128)S(1)} %get-tuple-element.16), channel_id=1, source_target_pairs={{1,2},{2,1},{5,6},{6,5},{9,10},{10,9},{13,14},{14,13},{17,18},{18,... | collective-permute-start | bytes 24584 | tf_op jit(solution)/shard_map/ppermute | solution.py:409
  129.7 15.9 %inner_force.3.partial = f32[4,2,2,4,128]{4,3,2,1,0:T(4,128)S(1)} custom-call(f32[7,2,2,4,128]{4,3,2,1,0:T(4,128)S(1)} %outer_force.2.own, f32[7,2,2,4,128]{4,3,2,1,0:T(4,128)S(1)} %collective-permute-done.6.slab_a, f32[7,2,2,4,128]{4,3,2,1,0:T(4,128)S(1)} %collective-permute-done.7.slab_b, f32[4,2,4,128]{3,2,1,0:T(4,128)S(1)} %get-tuple-element.14.rho), custom_call_target="tpu_custom_call" | custom-call | flops 17179869184 | bytes 524288 | tf_op jit(solution)/shard_map/inner_force/pallas_call | solution.py:362
  145.6 0.6 slice.3
  146.2 10.8 %outer_force.3 = (f32[3,2,2,4,128]{4,3,2,1,0:T(4,128)}, f32[3,2,2,4,128]{4,3,2,1,0:T(4,128)}) custom-call(f32[7,2,2,4,128]{4,3,2,1,0:T(4,128)S(1)} %outer_force.2.own, f32[7,2,2,4,128]{4,3,2,1,0:T(4,128)S(1)} %collective-permute-done.6.slab_a, f32[7,2,2,4,128]{4,3,2,1,0:T(4,128)S(1)} %collective-permute-done.7.slab_b, ...), custom_call_target="tpu_custom_call" | custom-call | flops 8589934592 | bytes 524288 | tf_op jit(solution)/shard_map/outer_force/pallas_call | solution.py:362
  (13 shorter events, 0.2 us)
Async XLA Ops:
  2.2 15.9 %collective-permute-start.1 = (f32[7,2,2,4,128]{4,3,2,1,0:T(4,128)S(1)}, f32[7,2,2,4,128]{4,3,2,1,0:T(4,128)S(1)}, u32[]{:S(2)}, u32[]{:S(2)}) collective-permute-start(f32[7,2,2,4,128]{4,3,2,1,0:T(4,128)S(1)} %pad_maximum_fusion.4.own), channel_id=1, source_target_pairs={{4,8},{8,4},{12,16},{16,12},{20,24},{24,20},{28,32},{32,28},{36,40... | collective-permute-start | bytes 172040 | tf_op jit(solution)/shard_map/ppermute | solution.py:409
  15.9 6.1 %collective-permute-start = (f32[7,2,2,4,128]{4,3,2,1,0:T(4,128)S(1)}, f32[7,2,2,4,128]{4,3,2,1,0:T(4,128)S(1)}, u32[]{:S(2)}, u32[]{:S(2)}) collective-permute-start(f32[7,2,2,4,128]{4,3,2,1,0:T(4,128)S(1)} %pad_maximum_fusion.4.own), channel_id=1, source_target_pairs={{0,4},{4,0},{8,12},{12,8},{16,20},{20,16},{24,28},{28,24},{32,36},... | collective-permute-start | bytes 172040 | tf_op jit(solution)/shard_map/ppermute | solution.py:404
  22.1 20.1 %collective-permute-start.2 = (f32[7,6,4,128]{3,2,1,0:T(4,128)S(1)}, f32[7,6,4,128]{3,2,1,0:T(4,128)S(1)}, u32[]{:S(2)}, u32[]{:S(2)}) collective-permute-start(f32[7,6,4,128]{3,2,1,0:T(4,128)S(1)} %pad_maximum_fusion), channel_id=1, source_target_pairs={{0,1},{1,0},{2,3},{3,2},{4,5},{5,4},{6,7},{7,6},{8,9},{9,8},{10,11... | collective-permute-start | bytes 258056 | tf_op jit(solution)/shard_map/ppermute | solution.py:404
  24.0 18.2 %collective-permute-start.3 = (f32[7,6,4,128]{3,2,1,0:T(4,128)S(1)}, f32[7,6,4,128]{3,2,1,0:T(4,128)S(1)}, u32[]{:S(2)}, u32[]{:S(2)}) collective-permute-start(f32[7,6,4,128]{3,2,1,0:T(4,128)S(1)} %pad_maximum_fusion.1), channel_id=1, source_target_pairs={{1,2},{2,1},{5,6},{6,5},{9,10},{10,9},{13,14},{14,13},{17,18},{18,... | collective-permute-start | bytes 258056 | tf_op jit(solution)/shard_map/ppermute | solution.py:409
  51.4 22.1 %collective-permute-start.4 = (f32[4,4,128]{2,1,0:T(4,128)S(1)}, f32[4,4,128]{2,1,0:T(4,128)S(1)}, u32[]{:S(2)}, u32[]{:S(2)}) collective-permute-start(f32[4,4,128]{2,1,0:T(4,128)S(1)} %get-tuple-element.12), channel_id=1, source_target_pairs={{0,1},{1,0},{2,3},{3,2},{4,5},{5,4},{6,7},{7,6},{8,9},{9,8},{10,11... | collective-permute-start | bytes 24584 | tf_op jit(solution)/shard_map/ppermute | solution.py:404
  53.3 20.2 %collective-permute-start.5 = (f32[4,4,128]{2,1,0:T(4,128)S(1)}, f32[4,4,128]{2,1,0:T(4,128)S(1)}, u32[]{:S(2)}, u32[]{:S(2)}) collective-permute-start(f32[4,4,128]{2,1,0:T(4,128)S(1)} %get-tuple-element.13), channel_id=1, source_target_pairs={{1,2},{2,1},{5,6},{6,5},{9,10},{10,9},{13,14},{14,13},{17,18},{18,... | collective-permute-start | bytes 24584 | tf_op jit(solution)/shard_map/ppermute | solution.py:409
  83.7 10.3 %collective-permute-start.7 = (f32[7,2,2,4,128]{4,3,2,1,0:T(4,128)S(1)}, f32[7,2,2,4,128]{4,3,2,1,0:T(4,128)S(1)}, u32[]{:S(2)}, u32[]{:S(2)}) collective-permute-start(f32[7,2,2,4,128]{4,3,2,1,0:T(4,128)S(1)} %outer_force.2.own), channel_id=1, source_target_pairs={{4,8},{8,4},{12,16},{16,12},{20,24},{24,20},{28,32},{32,28},{36,40... | collective-permute-start | bytes 172040 | tf_op jit(solution)/shard_map/ppermute | solution.py:409
  88.0 6.1 %collective-permute-start.6 = (f32[7,2,2,4,128]{4,3,2,1,0:T(4,128)S(1)}, f32[7,2,2,4,128]{4,3,2,1,0:T(4,128)S(1)}, u32[]{:S(2)}, u32[]{:S(2)}) collective-permute-start(f32[7,2,2,4,128]{4,3,2,1,0:T(4,128)S(1)} %outer_force.2.own), channel_id=1, source_target_pairs={{0,4},{4,0},{8,12},{12,8},{16,20},{20,16},{24,28},{28,24},{32,36},... | collective-permute-start | bytes 172040 | tf_op jit(solution)/shard_map/ppermute | solution.py:404
  94.1 19.1 %collective-permute-start.8 = (f32[7,6,4,128]{3,2,1,0:T(4,128)S(1)}, f32[7,6,4,128]{3,2,1,0:T(4,128)S(1)}, u32[]{:S(2)}, u32[]{:S(2)}) collective-permute-start(f32[7,6,4,128]{3,2,1,0:T(4,128)S(1)} %pad_maximum_fusion.2), channel_id=1, source_target_pairs={{0,1},{1,0},{2,3},{3,2},{4,5},{5,4},{6,7},{7,6},{8,9},{9,8},{10,11... | collective-permute-start | bytes 258056 | tf_op jit(solution)/shard_map/ppermute | solution.py:404
  96.1 17.2 %collective-permute-start.9 = (f32[7,6,4,128]{3,2,1,0:T(4,128)S(1)}, f32[7,6,4,128]{3,2,1,0:T(4,128)S(1)}, u32[]{:S(2)}, u32[]{:S(2)}) collective-permute-start(f32[7,6,4,128]{3,2,1,0:T(4,128)S(1)} %pad_maximum_fusion.3), channel_id=1, source_target_pairs={{1,2},{2,1},{5,6},{6,5},{9,10},{10,9},{13,14},{14,13},{17,18},{18,... | collective-permute-start | bytes 258056 | tf_op jit(solution)/shard_map/ppermute | solution.py:409
  122.4 23.8 %collective-permute-start.10 = (f32[4,4,128]{2,1,0:T(4,128)S(1)}, f32[4,4,128]{2,1,0:T(4,128)S(1)}, u32[]{:S(2)}, u32[]{:S(2)}) collective-permute-start(f32[4,4,128]{2,1,0:T(4,128)S(1)} %get-tuple-element.15), channel_id=1, source_target_pairs={{0,1},{1,0},{2,3},{3,2},{4,5},{5,4},{6,7},{7,6},{8,9},{9,8},{10,11... | collective-permute-start | bytes 24584 | tf_op jit(solution)/shard_map/ppermute | solution.py:404
  124.4 21.8 %collective-permute-start.11 = (f32[4,4,128]{2,1,0:T(4,128)S(1)}, f32[4,4,128]{2,1,0:T(4,128)S(1)}, u32[]{:S(2)}, u32[]{:S(2)}) collective-permute-start(f32[4,4,128]{2,1,0:T(4,128)S(1)} %get-tuple-element.16), channel_id=1, source_target_pairs={{1,2},{2,1},{5,6},{6,5},{9,10},{10,9},{13,14},{14,13},{17,18},{18,... | collective-permute-start | bytes 24584 | tf_op jit(solution)/shard_map/ppermute | solution.py:409
